TPU v7x, 256 devices: a whole 4x4x8 slice. The times are simulated.
256 devices in a mesh: space: 64 (over z, x, core), inst: 4 (over y).
Axes of the slice: x: 4, y: 4, z: 8, core: 2. Of those that a mesh axis runs over, the one named last changes fastest.
Arguments:
- adjoint: float32 [8, 5, 131072], P('inst', None, 'space'), may hold values from -6 to 6
- jac_cell: float32 [8, 5, 5, 131072], P('inst', None, None, 'space'), may hold values from -2.5 to 2.5
- jac_left: float32 [8, 5, 5, 131072], P('inst', None, None, 'space'), may hold values from -2.5 to 2.5
- jac_right: float32 [8, 5, 5, 131072], P('inst', None, None, 'space'), may hold values from -2.5 to 2.5
- volume: float32 [131072], P('space'), may hold values from 0.5 to 2
- normals: float32 [3, 131072], P(None, 'space'), may hold values from -6 to 6
- surface: int32 [131072], P('space'), may hold values 0 or 1
- instance_map: int32 [8], replicated, may hold values from 0 to 7, each once
- mode_shapes: float32 [200, 3, 131072], P(None, None, 'space'), may hold values from -0.01953125 to 0.01953125
- damping: float32 [200], replicated, may hold values from 0.2 to 2
- modal_inverse: float32 [200, 200], replicated, may hold values from -2 to 3
Outputs:
- flow_residual: float32 [8, 5, 131072], P('inst', None, 'space')
- mesh_forcing: float32 [8, 3, 131072], P('inst', None, 'space')
- modal_adjoint: float32 [8, 200], P('inst')
All inputs are finite; a program needn't handle non-finite values. No bound on the sum of `surface` on one device may be relied on, other than what follows from the above.
Results may differ from a plain program's by a relative error of at most 0.000068.
Values sent between devices are 32-bit elements; how exact they have to be, the bound alone decides.
A program may use at most 64 MiB of HBM per device.

v0:
```python
import jax
import jax.numpy as jnp
from jax import lax
from jax.sharding import PartitionSpec as P


def padded_2(shard, sides, width):
    for axis, dim in sides:
        count, length = (lax.axis_size(axis), shard.shape[dim])
        up = [(i, (i + 1) % count) for i in range(count - 1)]
        down = [(j, i) for i, j in up]
        last = lax.slice_in_dim(shard, length - width, length, axis=dim)
        leading = lax.slice_in_dim(shard, 0, width, axis=dim)
        before = lax.ppermute(last, axis, up)
        after = lax.ppermute(leading, axis, down)
        shard = jnp.concatenate([before, shard, after], axis=dim)
    return shard


def coupling_matrix(instance_map):
    count = instance_map.shape[0]
    slots = instance_map.astype(jnp.float32)
    differ = slots[:, None] - slots[None, :]
    angle = jnp.pi * differ / count
    same = differ == 0
    sine = jnp.where(same, 1.0, jnp.sin(angle))
    return jnp.where(same, 0.0, 0.5 * jnp.cos(jnp.pi * differ) * jnp.cos(angle) / sine)


def shards(
    adjoint,
    jac_cell,
    jac_left,
    jac_right,
    volume,
    normals,
    surface,
    instance_map,
    mode_shapes,
    damping,
    modal_inverse,
):
    highest = lax.Precision.HIGHEST
    own_slots = adjoint.shape[0]
    modes = mode_shapes.shape[0]
    first_slot = lax.axis_index("inst") * own_slots
    coupling = coupling_matrix(instance_map)
    own_cols = lax.dynamic_slice_in_dim(coupling, first_slot, own_slots, 1)
    flow = jnp.einsum("sfec,sfc->sec", jac_cell, adjoint, precision=highest)
    from_left = jnp.einsum("sfec,sfc->sec", jac_left, adjoint, precision=highest)
    from_right = jnp.einsum("sfec,sfc->sec", jac_right, adjoint, precision=highest)
    stacked = jnp.stack([from_left, from_right])
    padded = padded_2(stacked, (("space", 3),), 1)
    flow = flow + padded[0, :, :, 2:] + padded[1, :, :, :-2]
    timed = jnp.einsum(
        "ab,aec->bec",
        own_cols,
        lax.all_gather(adjoint, "inst", axis=0, tiled=True),
        precision=highest,
    )
    flow = flow + volume[None, None, :] * timed
    walls = surface.astype(jnp.float32)
    force = (walls[None, :] * flow[:, 4, :])[:, None, :] * normals[None, :, :]
    shapes = mode_shapes.reshape(modes, -1)
    projected = lax.dot_general(
        force.reshape(own_slots, -1),
        shapes,
        (((1,), (1,)), ((), ())),
        precision=highest,
        preferred_element_type=jnp.float32,
    )
    summed = lax.psum(projected, "space")
    gathered = lax.all_gather(summed, "inst", axis=0, tiled=True)
    own_projected = lax.dynamic_slice_in_dim(gathered, first_slot, own_slots, 0)
    modal_rhs = own_projected + damping[None, :] * jnp.dot(own_cols.T, gathered, precision=highest)
    modal_adjoint = jnp.dot(modal_rhs, modal_inverse, precision=highest)
    expanded = jnp.dot(modal_adjoint, shapes, precision=highest).reshape(own_slots, 3, -1)
    mesh_forcing = walls[None, None, :] * expanded
    return (flow, mesh_forcing, modal_adjoint)


def solution(mesh):
    placed = (
        P("inst", None, "space"),
        P("inst", None, None, "space"),
        P("inst", None, None, "space"),
        P("inst", None, None, "space"),
        P("space"),
        P(None, "space"),
        P("space"),
        P(),
        P(None, None, "space"),
        P(),
        P(),
    )
    return jax.shard_map(
        shards,
        mesh=mesh,
        in_specs=placed,
        out_specs=(P("inst", None, "space"), P("inst", None, "space"), P("inst", None)),
        check_vma=False,
    )
```

profile of v0, /device:TPU:1, one launch (start us, length us, event | category | flops | bytes accessed | tf_op | source)
XLA Modules:
  0.0 173.6 jit_solution(5606615448060914393)
XLA Ops:
  0.6 0.0 copy-start
  0.6 0.0 copy-start.3
  0.7 2.1 %multiply_reduce_fusion.2 = (f32[2,2048,5]{1,0,2:T(2,128)S(1)}, f32[2,2048,5]{1,0,2:T(2,128)S(1)}, f32[2,2048,5]{1,0,2:T(2,128)S(1)}) fusion(f32[2,5,5,2048]{3,0,2,1:T(2,128)} %param.12, f32[2,2048,5]{1,0,2:T(2,128)} %bitcast.61, f32[2,5,5,2048]{3,0,2,1:T(2,128)} %param.13, f32[2,5,5,2048]{3,0,2,1:T(2,128)} %param.14), kind=kLoop, calls=%fused_computation.10 | loop fusion | flops 552960 | bytes 1556480 | tf_op jit(solution)/shard_map/sfec,sfc->sec/dot_general | solution.py:49
  2.8 0.1 pad_maximum_fusion.5
  2.9 4.5 %collective-permute-start.1 = (f32[2,2,5,1]{3,1,2,0:T(2,128)S(1)}, f32[2,2,5,1]{3,1,2,0:T(2,128)S(1)}, u32[]{:S(2)}, u32[]{:S(2)}) collective-permute-start(f32[2,2,5,1]{3,1,2,0:T(2,128)S(1)} %get-tuple-element.7), channel_id=1, source_target_pairs={{0,4},{4,8},{8,12},{12,16},{16,20},{20,24},{24,28},{28,32},{32,36}... | collective-permute-start | bytes 248 | tf_op jit(solution)/shard_map/ppermute | solution.py:14
  7.4 1.9 %collective-permute-start = (f32[2,2,5,1]{3,1,2,0:T(2,128)S(1)}, f32[2,2,5,1]{3,1,2,0:T(2,128)S(1)}, u32[]{:S(2)}, u32[]{:S(2)}) collective-permute-start(f32[2,2,5,1]{3,1,2,0:T(2,128)S(1)} %get-tuple-element.6), channel_id=1, source_target_pairs={{4,0},{8,4},{12,8},{16,12},{20,16},{24,20},{28,24},{32,28},{36,32}... | collective-permute-start | bytes 248 | tf_op jit(solution)/shard_map/ppermute | solution.py:15
  9.3 0.9 copy.16
  10.3 12.0 %all_gather.6 = f32[8,5,2048]{2,1,0:T(8,128)S(1)} all-gather(f32[2,5,2048]{2,1,0:T(8,128)S(1)} %copy.16), channel_id=1, replica_groups=mesh['space'=64,'inst'=4] {'inst'}, dimensions={0}, use_global_device_ids=true | all-gather | bytes 409600 | tf_op jit(solution)/shard_map/all_gather | solution.py:58
  22.2 0.7 convert_element_type.6
  22.9 0.1 fusion.21
  23.0 0.7 convert_element_type.7
  23.7 0.0 collective-permute-done.1
  23.7 0.0 collective-permute-done
  23.7 1.3 fusion.10
  25.0 0.0 copy-start.2
  25.1 5.8 %convolution_bitcast_fusion = f32[2,200]{1,0:T(2,128)S(1)} fusion(f32[200,3,2048]{2,0,1:T(8,128)} %param.19, f32[3,2048]{1,0:T(4,128)} %param.16, f32[2,2048]{1,0:T(2,128)S(1)} %fusion.18), kind=kOutput, calls=%fused_computation.6 | convolution fusion | flops 29503488 | bytes 4957760 | tf_op jit(solution)/shard_map/dot_general | solution.py:65
  30.8 128.9 %psum.7 = f32[2,200]{1,0:T(2,128)S(1)} all-reduce(f32[2,200]{1,0:T(2,128)S(1)} %convolution_bitcast_fusion), channel_id=1, replica_groups=mesh['space'=64,'inst'=4] {'space'}, use_global_device_ids=true, to_apply=%region_0.1 | all-reduce | flops 400 | bytes 3200 | tf_op jit(solution)/shard_map/psum | solution.py:72
  159.7 8.1 %all-gather = f32[4,2,200]{2,1,0:T(2,128)S(1)} all-gather(f32[1,2,200]{2,1,0:T(2,128)S(1)} %bitcast.66), channel_id=1, replica_groups=mesh['space'=64,'inst'=4] {'inst'}, dimensions={0}, use_global_device_ids=true | all-gather | bytes 8000 | tf_op jit(solution)/shard_map/all_gather | solution.py:73
  167.8 0.0 copy-done.3
  167.8 0.1 fusion.6
  168.0 0.0 copy-done
  168.0 0.2 fusion.33
  168.2 5.5 %fusion.3 = f32[2,3,2048]{2,0,1:T(2,128)} fusion(f32[2048]{0:T(1024)S(1)} %convert_element_type.7, f32[2,200]{1,0:T(2,128)S(1)} %fusion.33, f32[200,3,2048]{2,0,1:T(8,128)} %param.19), kind=kOutput, calls=%fused_computation.4 | convolution fusion | flops 29503488 | bytes 4974144 | tf_op jit(solution)/shard_map/dot_general | solution.py:77
  173.6 0.0 copy-done.2
  (4 shorter events, 0.0 us)
Async XLA Ops:
  0.6 167.3 %copy-start = (f32[200,200]{1,0:T(8,128)S(1)}, f32[200,200]{1,0:T(8,128)}, u32[]{:S(2)}) copy-start(f32[200,200]{1,0:T(8,128)} %param.21) | copy-start | bytes 480004
  0.6 167.2 %copy-start.3 = (f32[200]{0:T(256)S(1)}, f32[200]{0:T(256)}, u32[]{:S(2)}) copy-start(f32[200]{0:T(256)} %param.20) | copy-start | bytes 2404
  2.9 20.8 %collective-permute-start.1 = (f32[2,2,5,1]{3,1,2,0:T(2,128)S(1)}, f32[2,2,5,1]{3,1,2,0:T(2,128)S(1)}, u32[]{:S(2)}, u32[]{:S(2)}) collective-permute-start(f32[2,2,5,1]{3,1,2,0:T(2,128)S(1)} %get-tuple-element.7), channel_id=1, source_target_pairs={{0,4},{4,8},{8,12},{12,16},{16,20},{20,24},{24,28},{28,32},{32,36}... | collective-permute-start | bytes 248 | tf_op jit(solution)/shard_map/ppermute | solution.py:14
  7.4 16.3 %collective-permute-start = (f32[2,2,5,1]{3,1,2,0:T(2,128)S(1)}, f32[2,2,5,1]{3,1,2,0:T(2,128)S(1)}, u32[]{:S(2)}, u32[]{:S(2)}) collective-permute-start(f32[2,2,5,1]{3,1,2,0:T(2,128)S(1)} %get-tuple-element.6), channel_id=1, source_target_pairs={{4,0},{8,4},{12,8},{16,12},{20,16},{24,20},{28,24},{32,28},{36,32}... | collective-permute-start | bytes 248 | tf_op jit(solution)/shard_map/ppermute | solution.py:15
  25.0 148.6 %copy-start.2 = (f32[2,5,2048]{2,0,1:T(2,128)}, f32[2,5,2048]{2,0,1:T(2,128)S(1)}, u32[]{:S(2)}) copy-start(f32[2,5,2048]{2,0,1:T(2,128)S(1)} %fusion.10) | copy-start | bytes 245764
  168.2 5.5 %copy-start.1 = (f32[2,200]{1,0:T(2,128)}, f32[2,200]{1,0:T(2,128)S(1)}, u32[]{:S(2)}) copy-start(f32[2,200]{1,0:T(2,128)S(1)} %fusion.33) | copy-start | bytes 4804
where the time goes:
time: 176 us; the launch traced here: 174 us
  blocking collectives  149 us (85%)
  matrix products  12.8 us (7%)
  starting transfers between devices  6.43 us (4%)
  other arithmetic  3.69 us (2%)
    psum x1, blocking collectives, shards(): summed = lax.psum(projected, 'space')  129 us
    all_gather x1, blocking collectives, shards(): lax.all_gather(adjoint, 'inst', axis=0, tiled=True)  12 us
    all_gather x1, blocking collectives, shards(): gathered = lax.all_gather(summed, 'inst', axis=0, tiled=True)  8.07 us
    dot_general x1, matrix products, shards(): lax.dot_general(force.reshape(own_slots, -1), shapes, (((1,), (1,)), ((),...  5.76 us
    dot_general x1, matrix products, shards(): jnp.dot(modal_adjoint, shapes, precision=highest).reshape(own_slots, 3, -1)  5.45 us
    ppermute x1, starting transfers between devices, padded_2(): before = lax.ppermute(last, axis, up)  4.5 us
  transfers between devices with their start and end apart: 2, of which 0 were waited for; matrix products, arithmetic and copies ran while one was open for 1% of the time, Pallas kernels for 0%

commit v1 on v0

v1 whole, which is shorter than its diff:
```python
import jax
import jax.numpy as jnp
from jax import lax
from jax.experimental import pallas as pl
from jax.experimental.pallas import tpu as pltpu
from jax.sharding import PartitionSpec as P

MESH = pl.DeviceIdType.MESH
HIGHEST = lax.Precision.HIGHEST
F32 = jnp.float32

NZ, NX, NY, NC = 8, 4, 4, 2
TILES = NZ * NX * NC
CHIPS = NZ * NX
MODES = 200
GROUPS = MODES // 8
ROWS = 208
WIDE = 256
CT = 16
CHUNKS = 4
CJ = CT // CHUNKS
MB = 5
EJ = 4


def iota(shape, dim):
    return lax.broadcasted_iota(jnp.int32, shape, dim)


def next_cell(x):
    shape = x.shape
    rolled = pltpu.roll(x, 127, 1)
    carried = pltpu.roll(rolled, shape[0] - 2, 0)
    carried = jnp.where(iota(shape, 0) >= shape[0] - 2, 0.0, carried)
    return jnp.where(iota(shape, 1) == 127, carried, rolled)


def previous_cell(x):
    shape = x.shape
    rolled = pltpu.roll(x, 1, 1)
    carried = pltpu.roll(rolled, 2, 0)
    carried = jnp.where(iota(shape, 0) < 2, 0.0, carried)
    return jnp.where(iota(shape, 1) == 0, carried, rolled)


def coupling_of(differ):
    d = differ.astype(F32)
    angle = d * (jnp.pi / 8)
    same = differ == 0
    sine = jnp.where(same, 1.0, jnp.sin(angle))
    return jnp.where(same, 0.0, 0.5 * jnp.cos(jnp.pi * d) * jnp.cos(angle) / sine)


def kernel(
    adj_h, jc_h, jl_h, jr_h, vol_h, nrm_h, surf_h, imap_h, shp_h, damp_h, inv_h,
    flow_o, mesh_o, modal_o,
    adj, jac4, jac, vol, nrm, surf, imap, shp, damp, inv,
    ls, vol2, surf2, ng, wts, acc, fl, fr, fb, hmat,
    ma, abuf, vmsg, vbuf, xl, xp, mb, bbuf, rr, inv_t, coef,
    hl, hr,
    lsem, csem, ready,
    asend, arecv, vsend, vrecv, hsend, hrecv, gsend, grecv, bsend, brecv,
):
    space, y = lax.axis_index("space"), lax.axis_index("inst")
    core = lax.rem(space, NC)
    chip = space // NC
    x = lax.rem(chip, NX)
    z = chip // NX
    other = 1 - core

    def at(zz, xx, cc):
        return (zz * NX + xx) * NC + cc

    local = []

    def bring(src, dst, sem):
        copy = pltpu.make_async_copy(src, dst, sem)
        copy.start()
        local.append(copy)
        return copy

    c_adj = bring(adj_h, adj.at[y], lsem.at[0])
    c_j4 = [bring(j.at[:, 4], jac4.at[i], lsem.at[1 + i]) for i, j in enumerate((jc_h, jl_h, jr_h))]
    c_vol = bring(vol_h, vol, lsem.at[4])
    c_surf = bring(surf_h, surf, lsem.at[5])
    c_nrm = bring(nrm_h, nrm, lsem.at[6])
    c_shp = []
    for k in range(CHUNKS):
        part = pl.ds(k * CJ * 128, CJ * 128)
        copy = pltpu.make_async_copy(shp_h.at[:, :, part], shp.at[:, :, part], csem.at[k])
        copy.start()
        c_shp.append(copy)
    c_imap = bring(imap_h, imap, lsem.at[7])
    c_damp = bring(damp_h, damp, lsem.at[8])
    c_inv = bring(inv_h, inv, lsem.at[9])
    c_jac = [bring(j.at[:, pl.ds(0, 4)], jac.at[i], lsem.at[10 + i]) for i, j in enumerate((jc_h, jl_h, jr_h))]

    barrier = pltpu.get_barrier_semaphore()

    def greet(where, inst):
        pl.semaphore_signal(barrier, inc=1, device_id=(where, inst), device_id_type=MESH)

    for dy in range(1, NY):
        for cc in range(NC):
            greet(at(z, x, cc), lax.rem(y + dy, NY))
    for dx in range(1, NX):
        for cc in range(NC):
            greet(at(z, lax.rem(x + dx, NX), cc), y)
    for dz in range(1, NZ):
        for cc in range(NC):
            greet(at(lax.rem(z + dz, NZ), x, cc), y)
    greet(at(z, x, other), y)
    greet(lax.rem(chip + CHIPS - 1, CHIPS) * NC + 1, y)
    greet(lax.rem(chip + 1, CHIPS) * NC, y)
    greeted = (NY - 1) * NC + (NX - 1) * NC + (NZ - 1) * NC + 3

    ma[...] = jnp.zeros_like(ma)
    vmsg[...] = jnp.zeros_like(vmsg)
    acc[...] = jnp.zeros_like(acc)

    c_vol.wait()
    c_surf.wait()
    c_nrm.wait()
    walls = surf[...].astype(F32)
    for s in range(2):
        vol2[pl.ds(s, CT, stride=2), :] = vol[...]
        surf2[pl.ds(s, CT, stride=2), :] = walls
    for d in range(3):
        for j in range(CT):
            ng[d, pl.ds(j, 1), :] = nrm[pl.ds(d, 1), pl.ds(128 * j, 128)]
    for d in range(3):
        ng[d] = ng[d] * walls
    c_adj.wait()
    for c in c_j4:
        c.wait()

    def combine(j, e):
        total = j[0, e] * adj[y, 0]
        for f in range(1, 5):
            total = total + j[f, e] * adj[y, f]
        return total

    def direct4(i):
        total = jac4[i, 0] * adj[y, 0]
        for f in range(1, 5):
            total = total + jac4[i, f] * adj[y, f]
        return total

    left4, right4 = direct4(1), direct4(2)
    fl[4] = left4
    fr[4] = right4
    base4 = direct4(0) + next_cell(left4) + previous_cell(right4)
    fb[4] = base4
    ls[0] = base4
    ls[1] = vol2[...] * adj[y, 4]
    for r in range(4):
        rows = ls[r // 2, pl.ds(r % 2, CT, stride=2), :]
        for d in range(3):
            wts[r, pl.ds(d * CT, CT), :] = rows * ng[d]
    lane8, sub8 = iota((8, 128), 1), iota((8, 128), 0)
    first = jnp.where(lane8 == 0, left4[0:8], 0.0)
    last = jnp.where(lane8 == 127, right4[24:32], 0.0)
    for s in range(2):
        edge = jnp.where(sub8 == 0, pltpu.roll(first, (8 - s) % 8, 0), 0.0)
        edge = edge + jnp.where(sub8 == 1, pltpu.roll(last, 3 - s, 0), 0.0)
        acc[s, pl.ds(MODES, 8), :] = edge

    for k in range(CHUNKS):
        c_shp[k].wait()

        def block(g, carry, k=k):
            row = pl.multiple_of(g * (8 * MB), 8)
            sums = [[acc[r, pl.ds(row + 8 * i, 8), :] for i in range(MB)] for r in range(4)]
            for d in range(3):
                for jj in range(CJ):
                    j = k * CJ + jj
                    weight = [wts[r, pl.ds(d * CT + j, 8, stride=0), :] for r in range(4)]
                    for i in range(MB):
                        tile = shp[d, pl.ds(row + 8 * i, 8), pl.ds(128 * j, 128)]
                        for r in range(4):
                            sums[r][i] = sums[r][i] + weight[r] * tile
            for r in range(4):
                for i in range(MB):
                    acc[r, pl.ds(row + 8 * i, 8), :] = sums[r][i]
            return carry

        lax.fori_loop(0, GROUPS // MB, block, 0)
    ends = ((0, 0), (CT - 1, 127))
    for v, (j, lane) in enumerate(ends):
        total = None
        for d in range(3):
            g = jnp.where(iota((1, 128), 1) == lane, ng[d, pl.ds(j, 1), :], 0.0)
            term = shp[d, :, pl.ds(128 * j, 128)] * g
            total = term if total is None else total + term
        acc[4 + v, pl.ds(0, MODES), :] = total
    ones = jnp.ones((8, 128), F32)
    across = (((1,), (1,)), ((), ()))
    for r in range(6):
        summed = lax.dot_general(ones, acc[r], across, precision=HIGHEST, preferred_element_type=F32)
        if r < 4:
            ma[pl.ds(r, 1), pl.ds(0, ROWS)] = summed[0:1]
        else:
            vmsg[pl.ds(r - 4, 1), pl.ds(0, ROWS)] = summed[0:1]

    pl.semaphore_wait(barrier, greeted)
    for dx in range(1, NX):
        for cc in range(NC):
            pl.semaphore_signal(ready, inc=1, device_id=(at(z, lax.rem(x + dx, NX), cc), y), device_id_type=MESH)

    def send(src, dst, ssem, rsem, where, inst):
        copy = pltpu.make_async_remote_copy(
            src_ref=src, dst_ref=dst, send_sem=ssem, recv_sem=rsem, device_id=(where, inst), device_id_type=MESH
        )
        copy.start()
        return copy

    mine = y * NC + core
    sent_a = []
    for n in range(1, NY * NC):
        dy, dc = n // NC, n % NC
        cc = lax.rem(core + dc, NC)
        sent_a.append(send(ma, abuf.at[mine], asend.at[n], arecv.at[mine], at(z, x, cc), lax.rem(y + dy, NY)))
    sent_v = [send(vmsg, vbuf.at[core], vsend.at[0], vrecv.at[core], at(z, x, other), y)]
    outer = lax.rem(chip + 2 * core - 1 + CHIPS, CHIPS)
    slot = 3 - core
    for cc in range(NC):
        sent_v.append(send(vmsg, vbuf.at[slot], vsend.at[1 + cc], vrecv.at[slot], outer * NC + cc, y))
    sent_g = []
    for dy in range(1, NY):
        sent_g.append(send(adj.at[y], adj.at[y], gsend.at[dy], grecv.at[y], space, lax.rem(y + dy, NY)))
    abuf[pl.ds(mine, 1)] = ma[...][None]
    vbuf[pl.ds(core, 1)] = vmsg[...][None]

    for c in c_jac:
        c.wait()

    def component(e, carry):
        left, right = combine(jac.at[1], e), combine(jac.at[2], e)
        fl[e] = left
        fr[e] = right
        fb[e] = combine(jac.at[0], e) + next_cell(left) + previous_cell(right)
        return carry

    lax.fori_loop(0, 4, component, 0)
    before, after = lax.rem(space + TILES - 1, TILES), lax.rem(space + 1, TILES)
    sent_h = [
        send(fl.at[:, pl.ds(0, 8), :], hr, hsend.at[0], hrecv.at[0], before, y),
        send(fr.at[:, pl.ds(24, 8), :], hl, hsend.at[1], hrecv.at[1], after, y),
    ]

    c_imap.wait()
    c_damp.wait()
    c_inv.wait()
    eight = iota((8, 8), 0) == iota((8, 8), 1)
    slots = jnp.broadcast_to(imap[...], (8, 8))
    down = jnp.sum(jnp.where(eight, slots.astype(F32), 0.0), axis=1, keepdims=True)
    differ = jnp.broadcast_to(down, (8, 8)) - slots.astype(F32)
    hmat[...] = coupling_of(differ.astype(jnp.int32))
    h = hmat[...]
    own = 2 * y + core
    rows8 = iota((8, 8), 0)
    lanes8 = iota((8, 8), 1)
    own_h = jnp.sum(jnp.where(lanes8 == own, h, 0.0), axis=1, keepdims=True)
    inv_t[...] = inv[...].T

    for n in range(1, NY * NC):
        dy, dc = n // NC, n % NC
        src = lax.rem(y + dy, NY) * NC + lax.rem(core + dc, NC)
        pltpu.make_async_copy(ma, abuf.at[src], arecv.at[src]).wait()
    pltpu.make_async_copy(vmsg, vbuf.at[other], vrecv.at[other]).wait()
    for v in (2, 3):
        pltpu.make_async_copy(vmsg, vbuf.at[v], vrecv.at[v]).wait()
    for cc in range(NC):
        for yy in range(NY):
            xl[cc, pl.ds(2 * yy, 2), :] = abuf[yy * NC + cc, pl.ds(0, 2), :]
            xp[cc, pl.ds(2 * yy, 2), :] = abuf[yy * NC + cc, pl.ds(2, 2), :]
    has_before = jnp.where(chip > 0, 1.0, 0.0)
    has_after = jnp.where(chip < CHIPS - 1, 1.0, 0.0)
    proj = xl[0] + xl[1]
    edges = (
        (xl[0][:, 200:201] * has_before, vbuf[2, pl.ds(1, 1), :]),
        (xl[0][:, 201:202], vbuf[1, pl.ds(0, 1), :]),
        (xl[1][:, 200:201], vbuf[0, pl.ds(1, 1), :]),
        (xl[1][:, 201:202] * has_after, vbuf[3, pl.ds(0, 1), :]),
    )
    for amount, vector in edges:
        proj = proj + amount * vector
    late = xp[0] + xp[1]
    for a in range(8):
        proj = proj - h[:, a : a + 1] * late[a : a + 1, :]
    plain = jnp.sum(jnp.where(iota((8, WIDE), 0) == own, proj, 0.0), axis=0, keepdims=True)
    mixed = jnp.sum(own_h * proj, axis=0, keepdims=True)
    rhs = plain[:, 0:MODES] + damp[...] * mixed[:, 0:MODES]
    mb[...] = jnp.zeros_like(mb)
    mb[pl.ds(0, 1), :] = rhs[:, 0:128]
    mb[pl.ds(1, 1), pl.ds(0, MODES - 128)] = rhs[:, 128:MODES]

    pl.semaphore_wait(ready, (NX - 1) * NC)

    def send_b(n, carry):
        send(mb, bbuf.at[space], bsend.at[n], brecv.at[space], lax.rem(space + n, TILES), y)
        return carry

    lax.fori_loop(1, TILES, send_b, 0)
    bbuf[pl.ds(space, 1)] = mb[...][None]

    pltpu.make_async_copy(hr, hr, hrecv.at[0]).wait()
    pltpu.make_async_copy(hl, hl, hrecv.at[1]).wait()
    for dy in range(1, NY):
        src = lax.rem(y + dy, NY)
        pltpu.make_async_copy(adj.at[src], adj.at[src], grecv.at[src]).wait()
    parity = lax.rem(iota((8, 128), 0), 2)
    pick = [jnp.sum(jnp.where(lanes8 == 2 * y + s, h, 0.0), axis=1, keepdims=True) for s in range(2)]

    def entry(a, s):
        return jnp.broadcast_to(pick[s][a : a + 1, :], (8, 128))

    same = [jnp.where(parity == 0, entry(2 * yy, 0), entry(2 * yy + 1, 1)) for yy in range(NY)]
    cross = [jnp.where(parity == 0, entry(2 * yy + 1, 0), entry(2 * yy, 1)) for yy in range(NY)]
    follows = jnp.where(space < TILES - 1, 1.0, 0.0)
    leads = jnp.where(space > 0, 1.0, 0.0)

    def finish(e, carry):
        for q in range(4):
            part = pl.ds(8 * q, 8)
            timed = jnp.zeros((8, 128), F32)
            for yy in range(NY):
                here = adj[yy, e, part, :]
                swapped = jnp.where(parity == 0, pltpu.roll(here, 7, 0), pltpu.roll(here, 1, 0))
                timed = timed + here * same[yy] + swapped * cross[yy]
            total = fb[e, part, :] + vol2[part, :] * timed
            if q == 0:
                moved = pltpu.roll(pltpu.roll(hl[e], 1, 1), 2, 0)
                total = total + jnp.where((sub8 < 2) & (lane8 == 0), moved * leads, 0.0)
            if q == 3:
                moved = pltpu.roll(pltpu.roll(hr[e], 127, 1), 6, 0)
                total = total + jnp.where((sub8 >= 6) & (lane8 == 127), moved * follows, 0.0)
            flow_o[e, part, :] = total
        return carry

    lax.fori_loop(0, 5, finish, 0)
    for c in sent_a + sent_v + sent_g + sent_h:
        c.wait_send()

    def arrive(n, carry):
        src = lax.rem(space + n, TILES)
        pltpu.make_async_copy(mb, bbuf.at[src], brecv.at[src]).wait()
        return carry

    lax.fori_loop(1, TILES, arrive, 0)
    rr[...] = jnp.zeros_like(rr)
    for cc in range(NC):
        total = bbuf[cc]
        for n in range(1, CHIPS):
            total = total + bbuf[n * NC + cc]
        rr[pl.ds(cc, 1), pl.ds(0, 128)] = total[0:1]
        rr[pl.ds(cc, 1), pl.ds(128, 128)] = total[1:2]
    both = rr[:, pl.ds(0, MODES)]
    columns = lax.dot_general(inv_t[...], both, across, precision=HIGHEST, preferred_element_type=F32)
    for s in range(2):
        coef[s] = jnp.broadcast_to(columns[:, s : s + 1], (MODES, 128))

    def expand(n, carry):
        d = n // (CT // EJ)
        j0 = lax.rem(n, CT // EJ) * EJ
        sums = [[jnp.zeros((8, 128), F32) for _ in range(EJ)] for _ in range(2)]
        for g in range(GROUPS):
            c0, c1 = coef[0, pl.ds(8 * g, 8), :], coef[1, pl.ds(8 * g, 8), :]
            for i in range(EJ):
                tile = shp[d, pl.ds(8 * g, 8), pl.ds(pl.multiple_of((j0 + i) * 128, 128), 128)]
                sums[0][i] = sums[0][i] + c0 * tile
                sums[1][i] = sums[1][i] + c1 * tile
        for i in range(EJ):
            for s in range(2):
                row = 2 * (j0 + i) + s
                line = jnp.sum(sums[s][i], axis=0, keepdims=True)
                mesh_o[d, pl.ds(row, 1), :] = line * surf2[pl.ds(row, 1), :]
        return carry

    lax.fori_loop(0, 3 * (CT // EJ), expand, 0)
    modal = jnp.dot(both, inv[...], precision=HIGHEST, preferred_element_type=F32)
    modal_o[...] = modal[0:2]

    def drain(n, carry):
        pltpu.make_async_copy(mb, mb, bsend.at[n]).wait()
        return carry

    lax.fori_loop(1, TILES, drain, 0)


def shards(
    adjoint, jac_cell, jac_left, jac_right, volume, normals, surface, instance_map, mode_shapes, damping, modal_inverse
):
    def tiles(array):
        lead = array.shape[1:-1]
        n = len(lead)
        split = array.reshape((2,) + lead + (CT, 128))
        order = tuple(range(1, n + 1)) + (n + 1, 0, n + 2)
        return split.transpose(order).reshape(lead + (2 * CT, 128))

    def slots(array):
        lead = array.shape[0]
        return array.reshape(lead, CT, 2, 128).transpose(2, 0, 1, 3).reshape(2, lead, CT * 128)

    args = (
        tiles(adjoint),
        tiles(jac_cell),
        tiles(jac_left),
        tiles(jac_right),
        volume.reshape(CT, 128),
        normals,
        surface.reshape(CT, 128),
        instance_map.reshape(1, 8),
        mode_shapes.transpose(1, 0, 2),
        damping.reshape(1, MODES),
        modal_inverse,
    )
    vmem = pltpu.VMEM
    dma = pltpu.SemaphoreType.DMA
    flow, mesh, modal = pl.pallas_call(
        kernel,
        out_shape=(
            jax.ShapeDtypeStruct((5, 2 * CT, 128), F32),
            jax.ShapeDtypeStruct((3, 2 * CT, 128), F32),
            jax.ShapeDtypeStruct((2, MODES), F32),
        ),
        in_specs=[pl.BlockSpec(memory_space=pl.ANY)] * len(args),
        out_specs=[pl.BlockSpec(memory_space=pltpu.VMEM)] * 3,
        scratch_shapes=[
            vmem((NY, 5, 32, 128), F32),
            vmem((3, 5, 32, 128), F32),
            vmem((3, 5, 4, 32, 128), F32),
            vmem((CT, 128), F32),
            vmem((3, CT * 128), F32),
            vmem((CT, 128), jnp.int32),
            vmem((1, 8), jnp.int32),
            vmem((3, MODES, CT * 128), F32),
            vmem((1, MODES), F32),
            vmem((MODES, MODES), F32),
            vmem((2, 32, 128), F32),
            vmem((32, 128), F32),
            vmem((32, 128), F32),
            vmem((3, CT, 128), F32),
            vmem((4, 3 * CT, 128), F32),
            vmem((6, ROWS, 128), F32),
            vmem((5, 32, 128), F32),
            vmem((5, 32, 128), F32),
            vmem((5, 32, 128), F32),
            vmem((8, 8), F32),
            vmem((4, WIDE), F32),
            vmem((NY * NC, 4, WIDE), F32),
            vmem((2, WIDE), F32),
            vmem((4, 2, WIDE), F32),
            vmem((2, 8, WIDE), F32),
            vmem((2, 8, WIDE), F32),
            vmem((2, 128), F32),
            vmem((TILES, 2, 128), F32),
            vmem((8, WIDE), F32),
            vmem((MODES, MODES), F32),
            vmem((2, MODES, 128), F32),
            vmem((5, 8, 128), F32),
            vmem((5, 8, 128), F32),
            dma((13,)),
            dma((CHUNKS,)),
            pltpu.SemaphoreType.REGULAR,
            dma((NY * NC,)),
            dma((NY * NC,)),
            dma((3,)),
            dma((4,)),
            dma((2,)),
            dma((2,)),
            dma((NY,)),
            dma((NY,)),
            dma((TILES,)),
            dma((TILES,)),
        ],
        compiler_params=pltpu.CompilerParams(
            collective_id=0, has_side_effects=True, vmem_limit_bytes=48 * 1024 * 1024
        ),
    )(*args)
    return slots(flow), slots(mesh), modal


def solution(mesh):
    placed = (
        P("inst", None, "space"),
        P("inst", None, None, "space"),
        P("inst", None, None, "space"),
        P("inst", None, None, "space"),
        P("space"),
        P(None, "space"),
        P("space"),
        P(),
        P(None, None, "space"),
        P(),
        P(),
    )
    return jax.shard_map(
        shards,
        mesh=mesh,
        in_specs=placed,
        out_specs=(P("inst", None, "space"), P("inst", None, "space"), P("inst", None)),
        check_vma=False,
    )
```

time: 176 us -> 38 us (0.22); the launches traced: 174 us -> 37.6 us
  blocking collectives: 149 us -> 0 us
  Pallas kernels: 0 us -> 26.8 us
  matrix products: 12.8 us -> 0 us
  local copies, waits for them, and re-layouts: 0.98 us -> 10.1 us
  starting transfers between devices: 6.43 us -> 0 us
  other arithmetic: 3.69 us -> 0 us
    psum x1 -> x0, blocking collectives: 129 us -> none  [shards(): summed = lax.psum(projected, 'space')]
    pallas_call x0 -> x1, Pallas kernels: none -> 26.8 us  [shards(): pl.pallas_call(kernel, out_shape=(jax.ShapeDtypeStruct((5, 2 * CT, 128),...]
    all_gather x2 -> x0, blocking collectives: 20 us -> none  [the longest x1 12 us: shards(): lax.all_gather(adjoint, 'inst', axis=0, tiled=True)]
    dot_general x5 -> x0, matrix products: 12.8 us -> none  [the longest x1 5.76 us: shards(): lax.dot_general(force.reshape(own_slots, -1), shapes, (((1,), (1,)), ((),...]
    unnamed x10 -> x23, local copies, waits for them, and re-layouts: 0.98 us -> 10.1 us
    ppermute x2 -> x0, starting transfers between devices: 6.43 us -> none  [the longest x1 4.5 us: padded_2(): before = lax.ppermute(last, axis, up)]
    dot_general x1 -> x0, other arithmetic: 2.12 us -> none  [shards(): flow = jnp.einsum('sfec,sfc->sec', jac_cell, adjoint, precision=highest)]
  transfers between devices with their start and end apart: 2 -> 0, of which waited for: 0 -> 0; matrix products, arithmetic and copies ran while one was open for 1% -> 0% of each run, Pallas kernels for 0% -> 0%
where the time goes in v1:
time: 38 us; the launch traced here: 37.6 us
  Pallas kernels  26.8 us (71%)
  local copies, waits for them, and re-layouts  10.1 us (27%)
  between operations  0.66 us (2%)
    pallas_call x1, Pallas kernels, shards(): pl.pallas_call(kernel, out_shape=(jax.ShapeDtypeStruct((5, 2 * CT, 128),...  26.8 us
    unnamed x23, local copies, waits for them, and re-layouts  10.1 us

profile of v1, /device:TPU:1, one launch (start us, length us, event | category | flops | bytes accessed | tf_op | source)
XLA Modules:
  0.0 37.6 jit_solution(11282143888992350144)
XLA Ops:
  0.6 0.0 copy-start
  0.6 1.0 %copy-done = f32[2,5,5,2048]{3,0,2,1:T(2,128)S(1)} copy-done((f32[2,5,5,2048]{3,0,2,1:T(2,128)S(1)}, f32[2,5,5,2048]{3,0,2,1:T(2,128)}, u32[]{:S(2)}) %copy-start) | copy-done | bytes 409624
  1.6 0.0 copy-start.1
  1.6 1.0 %copy-done.1 = f32[2,5,5,2048]{3,0,2,1:T(2,128)S(1)} copy-done((f32[2,5,5,2048]{3,0,2,1:T(2,128)S(1)}, f32[2,5,5,2048]{3,0,2,1:T(2,128)}, u32[]{:S(2)}) %copy-start.1) | copy-done | bytes 409624
  2.6 0.0 copy-start.2
  2.6 1.0 %copy-done.2 = f32[2,5,5,2048]{3,0,2,1:T(2,128)S(1)} copy-done((f32[2,5,5,2048]{3,0,2,1:T(2,128)S(1)}, f32[2,5,5,2048]{3,0,2,1:T(2,128)}, u32[]{:S(2)}) %copy-start.2) | copy-done | bytes 409624
  3.6 0.0 copy-start.3
  3.6 0.9 %copy-done.3 = f32[200,200]{1,0:T(8,128)S(1)} copy-done((f32[200,200]{1,0:T(8,128)S(1)}, f32[200,200]{1,0:T(8,128)}, u32[]{:S(2)}) %copy-start.3) | copy-done | bytes 160024
  4.6 0.0 copy-start.4
  4.6 0.9 %copy-done.4 = f32[2,5,2048]{2,0,1:T(2,128)S(1)} copy-done((f32[2,5,2048]{2,0,1:T(2,128)S(1)}, f32[2,5,2048]{2,0,1:T(2,128)}, u32[]{:S(2)}) %copy-start.4) | copy-done | bytes 81944
  5.5 0.0 copy-start.5
  5.5 0.8 %copy-done.5 = f32[3,2048]{1,0:T(4,128)S(1)} copy-done((f32[3,2048]{1,0:T(4,128)S(1)}, f32[3,2048]{1,0:T(4,128)}, u32[]{:S(2)}) %copy-start.5) | copy-done | bytes 24600
  6.2 0.0 copy-start.6
  6.2 0.7 %copy-done.6 = f32[2048]{0:T(1024)S(1)} copy-done((f32[2048]{0:T(1024)S(1)}, f32[2048]{0:T(1024)}, u32[]{:S(2)}) %copy-start.6) | copy-done | bytes 8216
  6.9 0.0 copy-start.7
  6.9 0.7 %copy-done.7 = s32[2048]{0:T(1024)S(1)} copy-done((s32[2048]{0:T(1024)S(1)}, s32[2048]{0:T(1024)}, u32[]{:S(2)}) %copy-start.7) | copy-done | bytes 8216
  7.6 0.0 copy-start.8
  7.6 0.7 %copy-done.8 = f32[200]{0:T(256)S(1)} copy-done((f32[200]{0:T(256)S(1)}, f32[200]{0:T(256)}, u32[]{:S(2)}) %copy-start.8) | copy-done | bytes 824
  8.3 0.0 copy-start.9
  8.3 0.7 %copy-done.9 = s32[8]{0:T(128)S(1)} copy-done((s32[8]{0:T(128)S(1)}, s32[8]{0:T(128)}, u32[]{:S(2)}) %copy-start.9) | copy-done | bytes 56
  8.9 26.8 %shard_map.130 = (f32[5,32,128]{2,1,0:T(8,128)S(1)}, f32[3,32,128]{2,1,0:T(8,128)S(1)}, f32[2,200]{1,0:T(2,128)S(1)}) custom-call(f32[5,32,128]{2,1,0:T(8,128)S(1)} %bitcast.39, f32[5,5,32,128]{3,2,1,0:T(8,128)S(1)} %bitcast.35, f32[5,5,32,128]{3,2,1,0:T(8,128)S(1)} %bitcast.36, f32[5,5,32,128]{3,2,1,0:T(8,128)S(1)} %bitcast.37, f32[16,128]{1,0:T(8,128)S(1)} %bitcast.41, ...), custom_call_target="tpu_custom_call" | custom-call | tf_op jit(solution)/shard_map/pallas_call | solution.py:420
  35.8 0.6 %copy.23 = f32[2,5,2048]{2,0,1:T(2,128)} copy(f32[2,5,2048]{2,0,1:T(2,128)S(1)} %bitcast.38) | data formatting | bytes 163840
  36.4 0.6 %copy.24 = f32[2,3,2048]{2,0,1:T(2,128)} copy(f32[2,3,2048]{2,0,1:T(2,128)S(1)} %bitcast.40) | data formatting | bytes 98304
  37.0 0.6 %copy.25 = f32[2,200]{1,0:T(2,128)} copy(f32[2,200]{1,0:T(2,128)S(1)} %get-tuple-element.14) | data formatting | bytes 3200
Async XLA Ops:
  0.6 1.0 %copy-start = (f32[2,5,5,2048]{3,0,2,1:T(2,128)S(1)}, f32[2,5,5,2048]{3,0,2,1:T(2,128)}, u32[]{:S(2)}) copy-start(f32[2,5,5,2048]{3,0,2,1:T(2,128)} %param.12) | copy-start | bytes 1228804
  1.6 1.0 %copy-start.1 = (f32[2,5,5,2048]{3,0,2,1:T(2,128)S(1)}, f32[2,5,5,2048]{3,0,2,1:T(2,128)}, u32[]{:S(2)}) copy-start(f32[2,5,5,2048]{3,0,2,1:T(2,128)} %param.13) | copy-start | bytes 1228804
  2.6 1.0 %copy-start.2 = (f32[2,5,5,2048]{3,0,2,1:T(2,128)S(1)}, f32[2,5,5,2048]{3,0,2,1:T(2,128)}, u32[]{:S(2)}) copy-start(f32[2,5,5,2048]{3,0,2,1:T(2,128)} %param.14) | copy-start | bytes 1228804
  3.6 0.9 %copy-start.3 = (f32[200,200]{1,0:T(8,128)S(1)}, f32[200,200]{1,0:T(8,128)}, u32[]{:S(2)}) copy-start(f32[200,200]{1,0:T(8,128)} %inv_h.1) | copy-start | bytes 480004
  4.6 0.9 %copy-start.4 = (f32[2,5,2048]{2,0,1:T(2,128)S(1)}, f32[2,5,2048]{2,0,1:T(2,128)}, u32[]{:S(2)}) copy-start(f32[2,5,2048]{2,0,1:T(2,128)} %param.11) | copy-start | bytes 245764
  5.5 0.8 %copy-start.5 = (f32[3,2048]{1,0:T(4,128)S(1)}, f32[3,2048]{1,0:T(4,128)}, u32[]{:S(2)}) copy-start(f32[3,2048]{1,0:T(4,128)} %nrm_h.1) | copy-start | bytes 73732
  6.2 0.7 %copy-start.6 = (f32[2048]{0:T(1024)S(1)}, f32[2048]{0:T(1024)}, u32[]{:S(2)}) copy-start(f32[2048]{0:T(1024)} %param.15) | copy-start | bytes 24580
  6.9 0.7 %copy-start.7 = (s32[2048]{0:T(1024)S(1)}, s32[2048]{0:T(1024)}, u32[]{:S(2)}) copy-start(s32[2048]{0:T(1024)} %param.17) | copy-start | bytes 24580
  7.6 0.7 %copy-start.8 = (f32[200]{0:T(256)S(1)}, f32[200]{0:T(256)}, u32[]{:S(2)}) copy-start(f32[200]{0:T(256)} %param.20) | copy-start | bytes 2404
  8.3 0.7 %copy-start.9 = (s32[8]{0:T(128)S(1)}, s32[8]{0:T(128)}, u32[]{:S(2)}) copy-start(s32[8]{0:T(128)} %param.18) | copy-start | bytes 100

commit v2 on v1

--- a/solution.py
+++ b/solution.py
@@ -17,7 +17,8 @@
 ROWS = 208
 WIDE = 256
 CT = 16
-CHUNKS = 4
+CHUNKS = 8
+AHEAD = 4
 CJ = CT // CHUNKS
 MB = 5
 EJ = 4
@@ -84,16 +85,13 @@
     c_vol = bring(vol_h, vol, lsem.at[4])
     c_surf = bring(surf_h, surf, lsem.at[5])
     c_nrm = bring(nrm_h, nrm, lsem.at[6])
-    c_shp = []
-    for k in range(CHUNKS):
-        part = pl.ds(k * CJ * 128, CJ * 128)
-        copy = pltpu.make_async_copy(shp_h.at[:, :, part], shp.at[:, :, part], csem.at[k])
-        copy.start()
-        c_shp.append(copy)
-    c_imap = bring(imap_h, imap, lsem.at[7])
-    c_damp = bring(damp_h, damp, lsem.at[8])
-    c_inv = bring(inv_h, inv, lsem.at[9])
-    c_jac = [bring(j.at[:, pl.ds(0, 4)], jac.at[i], lsem.at[10 + i]) for i, j in enumerate((jc_h, jl_h, jr_h))]
+
+    def chunk(k):
+        part = pl.ds(pl.multiple_of(k * (CJ * 128), CJ * 128), CJ * 128)
+        return pltpu.make_async_copy(shp_h.at[:, :, part], shp.at[:, :, part], csem.at[k])
+
+    for k in range(AHEAD):
+        chunk(k).start()
 
     barrier = pltpu.get_barrier_semaphore()
 
@@ -165,18 +163,23 @@
         edge = edge + jnp.where(sub8 == 1, pltpu.roll(last, 3 - s, 0), 0.0)
         acc[s, pl.ds(MODES, 8), :] = edge
 
-    for k in range(CHUNKS):
-        c_shp[k].wait()
-
-        def block(g, carry, k=k):
+    def project(k, carry):
+        chunk(k).wait()
+
+        @pl.when(k + AHEAD < CHUNKS)
+        def _():
+            chunk(k + AHEAD).start()
+
+        def block(g, carry):
             row = pl.multiple_of(g * (8 * MB), 8)
             sums = [[acc[r, pl.ds(row + 8 * i, 8), :] for i in range(MB)] for r in range(4)]
             for d in range(3):
                 for jj in range(CJ):
                     j = k * CJ + jj
                     weight = [wts[r, pl.ds(d * CT + j, 8, stride=0), :] for r in range(4)]
+                    column = pl.ds(pl.multiple_of(128 * j, 128), 128)
                     for i in range(MB):
-                        tile = shp[d, pl.ds(row + 8 * i, 8), pl.ds(128 * j, 128)]
+                        tile = shp[d, pl.ds(row + 8 * i, 8), column]
                         for r in range(4):
                             sums[r][i] = sums[r][i] + weight[r] * tile
             for r in range(4):
@@ -184,7 +187,13 @@
                     acc[r, pl.ds(row + 8 * i, 8), :] = sums[r][i]
             return carry
 
-        lax.fori_loop(0, GROUPS // MB, block, 0)
+        return lax.fori_loop(0, GROUPS // MB, block, carry)
+
+    lax.fori_loop(0, CHUNKS, project, 0)
+    c_imap = bring(imap_h, imap, lsem.at[7])
+    c_damp = bring(damp_h, damp, lsem.at[8])
+    c_inv = bring(inv_h, inv, lsem.at[9])
+    c_jac = [bring(j.at[:, pl.ds(0, 4)], jac.at[i], lsem.at[10 + i]) for i, j in enumerate((jc_h, jl_h, jr_h))]
     ends = ((0, 0), (CT - 1, 127))
     for v, (j, lane) in enumerate(ends):
         total = None
@@ -216,8 +225,8 @@
 
     mine = y * NC + core
     sent_a = []
-    for n in range(1, NY * NC):
-        dy, dc = n // NC, n % NC
+    for dy, dc in ((2, 0), (2, 1), (1, 0), (3, 0), (1, 1), (3, 1), (0, 1)):
+        n = dy * NC + dc
         cc = lax.rem(core + dc, NC)
         sent_a.append(send(ma, abuf.at[mine], asend.at[n], arecv.at[mine], at(z, x, cc), lax.rem(y + dy, NY)))
     sent_v = [send(vmsg, vbuf.at[core], vsend.at[0], vrecv.at[core], at(z, x, other), y)]
@@ -297,11 +306,14 @@
 
     pl.semaphore_wait(ready, (NX - 1) * NC)
 
-    def send_b(n, carry):
-        send(mb, bbuf.at[space], bsend.at[n], brecv.at[space], lax.rem(space + n, TILES), y)
-        return carry
-
-    lax.fori_loop(1, TILES, send_b, 0)
+    def hops(offset):
+        dz, dx, _ = offset
+        return min(dz, NZ - dz) + min(dx, NX - dx)
+
+    offsets = [(dz, dx, dc) for dz in range(NZ) for dx in range(NX) for dc in range(NC)][1:]
+    for n, (dz, dx, dc) in enumerate(sorted(offsets, key=hops, reverse=True)):
+        where = at(lax.rem(z + dz, NZ), lax.rem(x + dx, NX), lax.rem(core + dc, NC))
+        send(mb, bbuf.at[space], bsend.at[n], brecv.at[space], where, y)
     bbuf[pl.ds(space, 1)] = mb[...][None]
 
     pltpu.make_async_copy(hr, hr, hrecv.at[0]).wait()
@@ -357,6 +369,8 @@
         rr[pl.ds(cc, 1), pl.ds(128, 128)] = total[1:2]
     both = rr[:, pl.ds(0, MODES)]
     columns = lax.dot_general(inv_t[...], both, across, precision=HIGHEST, preferred_element_type=F32)
+    modal = jnp.dot(both, inv[...], precision=HIGHEST, preferred_element_type=F32)
+    modal_o[...] = modal[0:2]
     for s in range(2):
         coef[s] = jnp.broadcast_to(columns[:, s : s + 1], (MODES, 128))
 
@@ -378,14 +392,20 @@
         return carry
 
     lax.fori_loop(0, 3 * (CT // EJ), expand, 0)
-    modal = jnp.dot(both, inv[...], precision=HIGHEST, preferred_element_type=F32)
-    modal_o[...] = modal[0:2]
 
     def drain(n, carry):
         pltpu.make_async_copy(mb, mb, bsend.at[n]).wait()
         return carry
 
-    lax.fori_loop(1, TILES, drain, 0)
+    lax.fori_loop(0, TILES - 1, drain, 0)
+
+
+def place(*refs):
+    copies = [pltpu.make_async_copy(refs[i], refs[3 + i], refs[6].at[i]) for i in range(3)]
+    for copy in copies:
+        copy.start()
+    for copy in copies:
+        copy.wait()
 
 
 def shards(
@@ -416,14 +436,11 @@
         modal_inverse,
     )
     vmem = pltpu.VMEM
+    results = ((5, 2 * CT, 128), (3, 2 * CT, 128), (2, MODES))
     dma = pltpu.SemaphoreType.DMA
     flow, mesh, modal = pl.pallas_call(
         kernel,
-        out_shape=(
-            jax.ShapeDtypeStruct((5, 2 * CT, 128), F32),
-            jax.ShapeDtypeStruct((3, 2 * CT, 128), F32),
-            jax.ShapeDtypeStruct((2, MODES), F32),
-        ),
+        out_shape=tuple(vmem(shape, F32) for shape in results),
         in_specs=[pl.BlockSpec(memory_space=pl.ANY)] * len(args),
         out_specs=[pl.BlockSpec(memory_space=pltpu.VMEM)] * 3,
         scratch_shapes=[
@@ -475,9 +492,16 @@
             dma((TILES,)),
         ],
         compiler_params=pltpu.CompilerParams(
-            collective_id=0, has_side_effects=True, vmem_limit_bytes=48 * 1024 * 1024
+            collective_id=0, has_side_effects=True, vmem_limit_bytes=56 * 1024 * 1024
         ),
     )(*args)
+    flow, mesh, modal = pl.pallas_call(
+        place,
+        out_shape=tuple(jax.ShapeDtypeStruct(shape, F32) for shape in results),
+        in_specs=[pl.BlockSpec(memory_space=pltpu.VMEM)] * 3,
+        out_specs=[pl.BlockSpec(memory_space=pltpu.HBM)] * 3,
+        scratch_shapes=[dma((3,))],
+    )(*(pltpu.with_memory_space_constraint(part, pltpu.VMEM) for part in (flow, mesh, modal)))
     return slots(flow), slots(mesh), modal
 
 

time: 38 us -> 28.2 us (0.74)
  local copies, waits for them, and re-layouts: 10.1 us -> 0 us
  Pallas kernels: 26.8 us -> 27.4 us
    unnamed x23 -> x0, local copies, waits for them, and re-layouts: 10.1 us -> none
    pallas_call x1 -> x2, Pallas kernels: 26.8 us -> 27.4 us  [the longest x1 26.7 us: shards(): pl.pallas_call(kernel, out_shape=tuple((vmem(shape, F32) for shape in res...]
where the time goes in v2:
time: 28.2 us; the launch traced here: 28.1 us
  Pallas kernels  27.4 us (97%)
  between operations  0.64 us (2%)
    pallas_call x1, Pallas kernels, shards(): pl.pallas_call(kernel, out_shape=tuple((vmem(shape, F32) for shape in res...  26.7 us
    pallas_call x1, Pallas kernels, shards(): pl.pallas_call(place, out_shape=tuple((jax.ShapeDtypeStruct(shape, F32) f...  0.68 us

profile of v2, /device:TPU:1, one launch (start us, length us, event | category | flops | bytes accessed | tf_op | source)
XLA Modules:
  0.0 28.1 jit_solution(11953264747810940596)
XLA Ops:
  0.6 26.7 %shard_map.130 = (f32[5,32,128]{2,1,0:T(8,128)S(1)}, f32[3,32,128]{2,1,0:T(8,128)S(1)}, f32[2,200]{1,0:T(2,128)S(1)}) custom-call(f32[5,32,128]{2,1,0:T(8,128)} %bitcast.39, f32[5,5,32,128]{3,2,1,0:T(8,128)} %bitcast.36, f32[5,5,32,128]{3,2,1,0:T(8,128)} %bitcast.37, f32[5,5,32,128]{3,2,1,0:T(8,128)} %bitcast.38, f32[16,128]{1,0:T(8,128)} %bitcast.40, ...), custom_call_target="tpu_custom_call" | custom-call | tf_op jit(solution)/shard_map/pallas_call | solution.py:441
  27.4 0.7 %shard_map.131 = (f32[5,32,128]{2,1,0:T(8,128)}, f32[3,32,128]{2,1,0:T(8,128)}, f32[2,200]{1,0:T(2,128)}) custom-call(f32[5,32,128]{2,1,0:T(8,128)S(1)} %get-tuple-element.9.refs_0_, f32[3,32,128]{2,1,0:T(8,128)S(1)} %get-tuple-element.10.refs_1_, f32[2,200]{1,0:T(2,128)S(1)} %get-tuple-element.11.refs_2_), custom_call_target="tpu_custom_call" | custom-call | tf_op jit(solution)/shard_map/pallas_call | solution.py:498

commit v3 on v2

--- a/solution.py
+++ b/solution.py
@@ -13,15 +13,19 @@
 TILES = NZ * NX * NC
 CHIPS = NZ * NX
 MODES = 200
-GROUPS = MODES // 8
 ROWS = 208
 WIDE = 256
 CT = 16
+CELLS = CT * 128
 CHUNKS = 8
-AHEAD = 4
-CJ = CT // CHUNKS
-MB = 5
-EJ = 4
+CW = CELLS // CHUNKS
+EW = 512
+BF16 = jnp.bfloat16
+
+
+def halves(value):
+    upper = value.astype(BF16).astype(F32)
+    return jnp.concatenate([upper, value - upper], axis=0).astype(BF16)
 
 
 def iota(shape, dim):
@@ -53,11 +57,11 @@
 
 
 def kernel(
-    adj_h, jc_h, jl_h, jr_h, vol_h, nrm_h, surf_h, imap_h, shp_h, damp_h, inv_h,
+    adj_h, adjw_h, jc_h, jl_h, jr_h, jcw_h, jlw_h, jrw_h, vol_h, volw_h, nrm_h, surf_h, imap_h, shp_h, damp_h, inv_h,
     flow_o, mesh_o, modal_o,
-    adj, jac4, jac, vol, nrm, surf, imap, shp, damp, inv,
-    ls, vol2, surf2, ng, wts, acc, fl, fr, fb, hmat,
-    ma, abuf, vmsg, vbuf, xl, xp, mb, bbuf, rr, inv_t, coef,
+    adj, adjw, jac4, jac, vol, volw, nrm, surf, imap, shp, damp, inv,
+    vol2, wf, w16, shi, slo, fl, fr, fb,
+    ma, abuf, vmsg, vbuf, xl, xp, mb, bbuf, rr, mm,
     hl, hr,
     lsem, csem, ready,
     asend, arecv, vsend, vrecv, hsend, hrecv, gsend, grecv, bsend, brecv,
@@ -72,25 +76,20 @@
     def at(zz, xx, cc):
         return (zz * NX + xx) * NC + cc
 
-    local = []
-
     def bring(src, dst, sem):
         copy = pltpu.make_async_copy(src, dst, sem)
         copy.start()
-        local.append(copy)
         return copy
 
-    c_adj = bring(adj_h, adj.at[y], lsem.at[0])
-    c_j4 = [bring(j.at[:, 4], jac4.at[i], lsem.at[1 + i]) for i, j in enumerate((jc_h, jl_h, jr_h))]
-    c_vol = bring(vol_h, vol, lsem.at[4])
-    c_surf = bring(surf_h, surf, lsem.at[5])
-    c_nrm = bring(nrm_h, nrm, lsem.at[6])
+    c_first = [bring(adjw_h, adjw, lsem.at[0])]
+    c_first += [bring(j.at[:, 4], jac4.at[i], lsem.at[1 + i]) for i, j in enumerate((jcw_h, jlw_h, jrw_h))]
+    c_first += [bring(volw_h, volw, lsem.at[4]), bring(surf_h, surf, lsem.at[5]), bring(nrm_h, nrm, lsem.at[6])]
 
     def chunk(k):
-        part = pl.ds(pl.multiple_of(k * (CJ * 128), CJ * 128), CJ * 128)
-        return pltpu.make_async_copy(shp_h.at[:, :, part], shp.at[:, :, part], csem.at[k])
-
-    for k in range(AHEAD):
+        part = pl.ds(pl.multiple_of(k * CW, CW), CW)
+        return pltpu.make_async_copy(shp_h.at[:, :, part], shp.at[:, pl.ds(0, MODES), part], csem.at[k])
+
+    for k in range(CHUNKS):
         chunk(k).start()
 
     barrier = pltpu.get_barrier_semaphore()
@@ -114,103 +113,68 @@
 
     ma[...] = jnp.zeros_like(ma)
     vmsg[...] = jnp.zeros_like(vmsg)
-    acc[...] = jnp.zeros_like(acc)
-
-    c_vol.wait()
-    c_surf.wait()
-    c_nrm.wait()
+    wf[...] = jnp.zeros_like(wf)
+    for d in range(3):
+        shp[d, pl.ds(MODES, ROWS - MODES), :] = jnp.zeros((ROWS - MODES, CELLS), F32)
+
+    for c in c_first:
+        c.wait()
+
+    def direct4(i):
+        total = jac4[i, 0] * adjw[0]
+        for f in range(1, 5):
+            total = total + jac4[i, f] * adjw[f]
+        return total
+
+    left4, right4 = direct4(1), direct4(2)
+    cell = iota((2, CELLS), 1)
+    base4 = direct4(0) + jnp.where(cell == CELLS - 1, 0.0, pltpu.roll(left4, CELLS - 1, 1))
+    base4 = base4 + jnp.where(cell == 0, 0.0, pltpu.roll(right4, 1, 1))
+    late4 = volw[...] * adjw[4]
     walls = surf[...].astype(F32)
-    for s in range(2):
-        vol2[pl.ds(s, CT, stride=2), :] = vol[...]
-        surf2[pl.ds(s, CT, stride=2), :] = walls
     for d in range(3):
-        for j in range(CT):
-            ng[d, pl.ds(j, 1), :] = nrm[pl.ds(d, 1), pl.ds(128 * j, 128)]
-    for d in range(3):
-        ng[d] = ng[d] * walls
-    c_adj.wait()
-    for c in c_j4:
-        c.wait()
-
-    def combine(j, e):
-        total = j[0, e] * adj[y, 0]
-        for f in range(1, 5):
-            total = total + j[f, e] * adj[y, f]
-        return total
-
-    def direct4(i):
-        total = jac4[i, 0] * adj[y, 0]
-        for f in range(1, 5):
-            total = total + jac4[i, f] * adj[y, f]
-        return total
-
-    left4, right4 = direct4(1), direct4(2)
-    fl[4] = left4
-    fr[4] = right4
-    base4 = direct4(0) + next_cell(left4) + previous_cell(right4)
-    fb[4] = base4
-    ls[0] = base4
-    ls[1] = vol2[...] * adj[y, 4]
-    for r in range(4):
-        rows = ls[r // 2, pl.ds(r % 2, CT, stride=2), :]
-        for d in range(3):
-            wts[r, pl.ds(d * CT, CT), :] = rows * ng[d]
-    lane8, sub8 = iota((8, 128), 1), iota((8, 128), 0)
-    first = jnp.where(lane8 == 0, left4[0:8], 0.0)
-    last = jnp.where(lane8 == 127, right4[24:32], 0.0)
-    for s in range(2):
-        edge = jnp.where(sub8 == 0, pltpu.roll(first, (8 - s) % 8, 0), 0.0)
-        edge = edge + jnp.where(sub8 == 1, pltpu.roll(last, 3 - s, 0), 0.0)
-        acc[s, pl.ds(MODES, 8), :] = edge
+        part = pl.ds(d * CELLS, CELLS)
+        g = nrm[pl.ds(d, 1), :] * walls
+        wf[pl.ds(0, 2), part] = base4 * g
+        wf[pl.ds(2, 2), part] = late4 * g
+        wf[pl.ds(4, 1), pl.ds(d * CELLS, 128)] = jnp.where(iota((1, 128), 1) == 0, g[:, 0:128], 0.0)
+        wf[pl.ds(5, 1), pl.ds((d + 1) * CELLS - 128, 128)] = jnp.where(iota((1, 128), 1) == 127, g[:, CELLS - 128 :], 0.0)
+    w16[...] = halves(wf[...])
+
+    across = (((1,), (1,)), ((), ()))
 
     def project(k, carry):
         chunk(k).wait()
-
-        @pl.when(k + AHEAD < CHUNKS)
-        def _():
-            chunk(k + AHEAD).start()
-
-        def block(g, carry):
-            row = pl.multiple_of(g * (8 * MB), 8)
-            sums = [[acc[r, pl.ds(row + 8 * i, 8), :] for i in range(MB)] for r in range(4)]
-            for d in range(3):
-                for jj in range(CJ):
-                    j = k * CJ + jj
-                    weight = [wts[r, pl.ds(d * CT + j, 8, stride=0), :] for r in range(4)]
-                    column = pl.ds(pl.multiple_of(128 * j, 128), 128)
-                    for i in range(MB):
-                        tile = shp[d, pl.ds(row + 8 * i, 8), column]
-                        for r in range(4):
-                            sums[r][i] = sums[r][i] + weight[r] * tile
-            for r in range(4):
-                for i in range(MB):
-                    acc[r, pl.ds(row + 8 * i, 8), :] = sums[r][i]
-            return carry
-
-        return lax.fori_loop(0, GROUPS // MB, block, carry)
-
-    lax.fori_loop(0, CHUNKS, project, 0)
+        high, low = carry
+        for d in range(3):
+            part = pl.ds(pl.multiple_of(k * CW, CW), CW)
+            tile = shp[d, :, part]
+            upper = tile.astype(BF16)
+            lower = (tile - upper.astype(F32)).astype(BF16)
+            shi[d, :, part] = upper
+            slo[d, :, part] = lower
+            weight = w16[:, pl.ds(pl.multiple_of(d * CELLS + k * CW, CW), CW)]
+            high = high + lax.dot_general(weight, upper, across, preferred_element_type=F32)
+            low = low + lax.dot_general(weight, lower, across, preferred_element_type=F32)
+        return high, low
+
+    nothing = jnp.zeros((16, ROWS), F32)
+    high, low = lax.fori_loop(0, CHUNKS, project, (nothing, nothing))
+    both = high + low
+    summed = both[0:8] + both[8:16]
+    ma[:, pl.ds(0, ROWS)] = summed[0:4]
+    vmsg[:, pl.ds(0, ROWS)] = summed[4:6]
+    lanes = iota((2, 128), 1)
+    tail = ma[pl.ds(0, 2), pl.ds(128, 128)]
+    tail = jnp.where(lanes == MODES - 128, left4[:, 0:1], tail)
+    tail = jnp.where(lanes == MODES + 1 - 128, right4[:, CELLS - 1 :], tail)
+    ma[pl.ds(0, 2), pl.ds(128, 128)] = tail
+
     c_imap = bring(imap_h, imap, lsem.at[7])
     c_damp = bring(damp_h, damp, lsem.at[8])
     c_inv = bring(inv_h, inv, lsem.at[9])
-    c_jac = [bring(j.at[:, pl.ds(0, 4)], jac.at[i], lsem.at[10 + i]) for i, j in enumerate((jc_h, jl_h, jr_h))]
-    ends = ((0, 0), (CT - 1, 127))
-    for v, (j, lane) in enumerate(ends):
-        total = None
-        for d in range(3):
-            g = jnp.where(iota((1, 128), 1) == lane, ng[d, pl.ds(j, 1), :], 0.0)
-            term = shp[d, :, pl.ds(128 * j, 128)] * g
-            total = term if total is None else total + term
-        acc[4 + v, pl.ds(0, MODES), :] = total
-    ones = jnp.ones((8, 128), F32)
-    across = (((1,), (1,)), ((), ()))
-    for r in range(6):
-        summed = lax.dot_general(ones, acc[r], across, precision=HIGHEST, preferred_element_type=F32)
-        if r < 4:
-            ma[pl.ds(r, 1), pl.ds(0, ROWS)] = summed[0:1]
-        else:
-            vmsg[pl.ds(r - 4, 1), pl.ds(0, ROWS)] = summed[0:1]
-
+    c_jac = [bring(j, jac.at[i], lsem.at[10 + i]) for i, j in enumerate((jc_h, jl_h, jr_h))]
+    c_jac += [bring(adj_h, adj.at[y], lsem.at[13]), bring(vol_h, vol, lsem.at[14])]
     pl.semaphore_wait(barrier, greeted)
     for dx in range(1, NX):
         for cc in range(NC):
@@ -234,14 +198,22 @@
     slot = 3 - core
     for cc in range(NC):
         sent_v.append(send(vmsg, vbuf.at[slot], vsend.at[1 + cc], vrecv.at[slot], outer * NC + cc, y))
+    abuf[pl.ds(mine, 1)] = ma[...][None]
+    vbuf[pl.ds(core, 1)] = vmsg[...][None]
+
+    for c in c_jac:
+        c.wait()
+    for s in range(2):
+        vol2[pl.ds(s, CT, stride=2), :] = vol[...]
     sent_g = []
     for dy in range(1, NY):
         sent_g.append(send(adj.at[y], adj.at[y], gsend.at[dy], grecv.at[y], space, lax.rem(y + dy, NY)))
-    abuf[pl.ds(mine, 1)] = ma[...][None]
-    vbuf[pl.ds(core, 1)] = vmsg[...][None]
-
-    for c in c_jac:
-        c.wait()
+
+    def combine(j, e):
+        total = j[0, e] * adj[y, 0]
+        for f in range(1, 5):
+            total = total + j[f, e] * adj[y, f]
+        return total
 
     def component(e, carry):
         left, right = combine(jac.at[1], e), combine(jac.at[2], e)
@@ -250,7 +222,7 @@
         fb[e] = combine(jac.at[0], e) + next_cell(left) + previous_cell(right)
         return carry
 
-    lax.fori_loop(0, 4, component, 0)
+    lax.fori_loop(0, 5, component, 0)
     before, after = lax.rem(space + TILES - 1, TILES), lax.rem(space + 1, TILES)
     sent_h = [
         send(fl.at[:, pl.ds(0, 8), :], hr, hsend.at[0], hrecv.at[0], before, y),
@@ -264,13 +236,10 @@
     slots = jnp.broadcast_to(imap[...], (8, 8))
     down = jnp.sum(jnp.where(eight, slots.astype(F32), 0.0), axis=1, keepdims=True)
     differ = jnp.broadcast_to(down, (8, 8)) - slots.astype(F32)
-    hmat[...] = coupling_of(differ.astype(jnp.int32))
-    h = hmat[...]
+    h = coupling_of(differ.astype(jnp.int32))
     own = 2 * y + core
-    rows8 = iota((8, 8), 0)
     lanes8 = iota((8, 8), 1)
     own_h = jnp.sum(jnp.where(lanes8 == own, h, 0.0), axis=1, keepdims=True)
-    inv_t[...] = inv[...].T
 
     for n in range(1, NY * NC):
         dy, dc = n // NC, n % NC
@@ -314,14 +283,16 @@
     for n, (dz, dx, dc) in enumerate(sorted(offsets, key=hops, reverse=True)):
         where = at(lax.rem(z + dz, NZ), lax.rem(x + dx, NX), lax.rem(core + dc, NC))
         send(mb, bbuf.at[space], bsend.at[n], brecv.at[space], where, y)
-    bbuf[pl.ds(space, 1)] = mb[...][None]
-
+
+    rr[...] = jnp.zeros_like(rr)
+    mm[...] = jnp.zeros_like(mm)
     pltpu.make_async_copy(hr, hr, hrecv.at[0]).wait()
     pltpu.make_async_copy(hl, hl, hrecv.at[1]).wait()
     for dy in range(1, NY):
         src = lax.rem(y + dy, NY)
         pltpu.make_async_copy(adj.at[src], adj.at[src], grecv.at[src]).wait()
-    parity = lax.rem(iota((8, 128), 0), 2)
+    lane8, sub8 = iota((8, 128), 1), iota((8, 128), 0)
+    parity = lax.rem(sub8, 2)
     pick = [jnp.sum(jnp.where(lanes8 == 2 * y + s, h, 0.0), axis=1, keepdims=True) for s in range(2)]
 
     def entry(a, s):
@@ -354,44 +325,29 @@
     for c in sent_a + sent_v + sent_g + sent_h:
         c.wait_send()
 
-    def arrive(n, carry):
-        src = lax.rem(space + n, TILES)
+    own_sum, other_sum = mb[...], jnp.zeros((2, 128), F32)
+    for dz, dx, dc in sorted(offsets, key=hops):
+        src = at(lax.rem(z + dz, NZ), lax.rem(x + dx, NX), lax.rem(core + dc, NC))
         pltpu.make_async_copy(mb, bbuf.at[src], brecv.at[src]).wait()
-        return carry
-
-    lax.fori_loop(1, TILES, arrive, 0)
-    rr[...] = jnp.zeros_like(rr)
-    for cc in range(NC):
-        total = bbuf[cc]
-        for n in range(1, CHIPS):
-            total = total + bbuf[n * NC + cc]
-        rr[pl.ds(cc, 1), pl.ds(0, 128)] = total[0:1]
-        rr[pl.ds(cc, 1), pl.ds(128, 128)] = total[1:2]
-    both = rr[:, pl.ds(0, MODES)]
-    columns = lax.dot_general(inv_t[...], both, across, precision=HIGHEST, preferred_element_type=F32)
-    modal = jnp.dot(both, inv[...], precision=HIGHEST, preferred_element_type=F32)
+        if dc == 0:
+            own_sum = own_sum + bbuf[src]
+        else:
+            other_sum = other_sum + bbuf[src]
+    even = jnp.broadcast_to(core, (2, 128)) == 0
+    for row, total in enumerate((jnp.where(even, own_sum, other_sum), jnp.where(even, other_sum, own_sum))):
+        rr[pl.ds(row, 1), pl.ds(0, 128)] = total[0:1]
+        rr[pl.ds(row, 1), pl.ds(128, 128)] = total[1:2]
+    modal = jnp.dot(rr[:, pl.ds(0, MODES)], inv[...], precision=HIGHEST, preferred_element_type=F32)
     modal_o[...] = modal[0:2]
-    for s in range(2):
-        coef[s] = jnp.broadcast_to(columns[:, s : s + 1], (MODES, 128))
-
-    def expand(n, carry):
-        d = n // (CT // EJ)
-        j0 = lax.rem(n, CT // EJ) * EJ
-        sums = [[jnp.zeros((8, 128), F32) for _ in range(EJ)] for _ in range(2)]
-        for g in range(GROUPS):
-            c0, c1 = coef[0, pl.ds(8 * g, 8), :], coef[1, pl.ds(8 * g, 8), :]
-            for i in range(EJ):
-                tile = shp[d, pl.ds(8 * g, 8), pl.ds(pl.multiple_of((j0 + i) * 128, 128), 128)]
-                sums[0][i] = sums[0][i] + c0 * tile
-                sums[1][i] = sums[1][i] + c1 * tile
-        for i in range(EJ):
-            for s in range(2):
-                row = 2 * (j0 + i) + s
-                line = jnp.sum(sums[s][i], axis=0, keepdims=True)
-                mesh_o[d, pl.ds(row, 1), :] = line * surf2[pl.ds(row, 1), :]
-        return carry
-
-    lax.fori_loop(0, 3 * (CT // EJ), expand, 0)
+    mm[:, pl.ds(0, MODES)] = modal
+    lead = halves(mm[:, pl.ds(0, ROWS)])
+    plain_dot = (((1,), (0,)), ((), ()))
+    for d in range(3):
+        for k in range(CELLS // EW):
+            part = pl.ds(k * EW, EW)
+            spread = lax.dot_general(lead, shi[d, :, part], plain_dot, preferred_element_type=F32)
+            spread = spread + lax.dot_general(lead, slo[d, :, part], plain_dot, preferred_element_type=F32)
+            mesh_o[d, :, part] = (spread[0:8] + spread[8:16])[0:2] * surf[:, part].astype(F32)
 
     def drain(n, carry):
         pltpu.make_async_copy(mb, mb, bsend.at[n]).wait()
@@ -422,21 +378,29 @@
         lead = array.shape[0]
         return array.reshape(lead, CT, 2, 128).transpose(2, 0, 1, 3).reshape(2, lead, CT * 128)
 
+    def wide(array):
+        return jnp.moveaxis(array, 0, -2)
+
     args = (
         tiles(adjoint),
+        wide(adjoint),
         tiles(jac_cell),
         tiles(jac_left),
         tiles(jac_right),
+        wide(jac_cell),
+        wide(jac_left),
+        wide(jac_right),
         volume.reshape(CT, 128),
+        volume.reshape(1, CELLS),
         normals,
-        surface.reshape(CT, 128),
+        surface.reshape(1, CELLS),
         instance_map.reshape(1, 8),
         mode_shapes.transpose(1, 0, 2),
         damping.reshape(1, MODES),
         modal_inverse,
     )
     vmem = pltpu.VMEM
-    results = ((5, 2 * CT, 128), (3, 2 * CT, 128), (2, MODES))
+    results = ((5, 2 * CT, 128), (3, 2, CELLS), (2, MODES))
     dma = pltpu.SemaphoreType.DMA
     flow, mesh, modal = pl.pallas_call(
         kernel,
@@ -445,25 +409,25 @@
         out_specs=[pl.BlockSpec(memory_space=pltpu.VMEM)] * 3,
         scratch_shapes=[
             vmem((NY, 5, 32, 128), F32),
-            vmem((3, 5, 32, 128), F32),
-            vmem((3, 5, 4, 32, 128), F32),
+            vmem((5, 2, CELLS), F32),
+            vmem((3, 5, 2, CELLS), F32),
+            vmem((3, 5, 5, 32, 128), F32),
             vmem((CT, 128), F32),
-            vmem((3, CT * 128), F32),
-            vmem((CT, 128), jnp.int32),
+            vmem((1, CELLS), F32),
+            vmem((3, CELLS), F32),
+            vmem((1, CELLS), jnp.int32),
             vmem((1, 8), jnp.int32),
-            vmem((3, MODES, CT * 128), F32),
+            vmem((3, ROWS, CELLS), F32),
             vmem((1, MODES), F32),
             vmem((MODES, MODES), F32),
-            vmem((2, 32, 128), F32),
             vmem((32, 128), F32),
-            vmem((32, 128), F32),
-            vmem((3, CT, 128), F32),
-            vmem((4, 3 * CT, 128), F32),
-            vmem((6, ROWS, 128), F32),
+            vmem((8, 3 * CELLS), F32),
+            vmem((16, 3 * CELLS), BF16),
+            vmem((3, ROWS, CELLS), BF16),
+            vmem((3, ROWS, CELLS), BF16),
             vmem((5, 32, 128), F32),
             vmem((5, 32, 128), F32),
             vmem((5, 32, 128), F32),
-            vmem((8, 8), F32),
             vmem((4, WIDE), F32),
             vmem((NY * NC, 4, WIDE), F32),
             vmem((2, WIDE), F32),
@@ -473,11 +437,10 @@
             vmem((2, 128), F32),
             vmem((TILES, 2, 128), F32),
             vmem((8, WIDE), F32),
-            vmem((MODES, MODES), F32),
-            vmem((2, MODES, 128), F32),
+            vmem((8, WIDE), F32),
             vmem((5, 8, 128), F32),
             vmem((5, 8, 128), F32),
-            dma((13,)),
+            dma((15,)),
             dma((CHUNKS,)),
             pltpu.SemaphoreType.REGULAR,
             dma((NY * NC,)),
@@ -502,7 +465,7 @@
         out_specs=[pl.BlockSpec(memory_space=pltpu.HBM)] * 3,
         scratch_shapes=[dma((3,))],
     )(*(pltpu.with_memory_space_constraint(part, pltpu.VMEM) for part in (flow, mesh, modal)))
-    return slots(flow), slots(mesh), modal
+    return slots(flow), mesh.transpose(1, 0, 2), modal
 
 
 def solution(mesh):

time: 28.2 us -> 25.9 us (0.918)
  Pallas kernels: 27.4 us -> 25.1 us
    pallas_call x1, Pallas kernels: 26.7 us -> 24.5 us  [shards(): pl.pallas_call(kernel, out_shape=tuple((vmem(shape, F32) for shape in res...]
where the time goes in v3:
time: 25.9 us; the launch traced here: 25.8 us
  Pallas kernels  25.1 us (97%)
  between operations  0.64 us (2%)
    pallas_call x1, Pallas kernels, shards(): pl.pallas_call(kernel, out_shape=tuple((vmem(shape, F32) for shape in res...  24.5 us
    pallas_call x1, Pallas kernels, shards(): pl.pallas_call(place, out_shape=tuple((jax.ShapeDtypeStruct(shape, F32) f...  0.68 us

profile of v3, /device:TPU:1, one launch (start us, length us, event | category | flops | bytes accessed | tf_op | source)
XLA Modules:
  0.0 25.8 jit_solution(367895950648780733)
XLA Ops:
  0.6 24.5 %shard_map.130 = (f32[5,32,128]{2,1,0:T(8,128)S(1)}, f32[3,2,2048]{2,1,0:T(2,128)S(1)}, f32[2,200]{1,0:T(2,128)S(1)}) custom-call(f32[5,32,128]{2,1,0:T(8,128)} %bitcast.43, f32[5,2,2048]{2,1,0:T(2,128)} %bitcast.44, f32[5,5,32,128]{3,2,1,0:T(8,128)} %bitcast.37, f32[5,5,32,128]{3,2,1,0:T(8,128)} %bitcast.39, f32[5,5,32,128]{3,2,1,0:T(8,128)} %bitcast.41, ...), custom_call_target="tpu_custom_call" | custom-call | tf_op jit(solution)/shard_map/pallas_call | solution.py:405
  25.1 0.7 %shard_map.131 = (f32[5,32,128]{2,1,0:T(8,128)}, f32[3,2,2048]{2,1,0:T(2,128)}, f32[2,200]{1,0:T(2,128)}) custom-call(f32[5,32,128]{2,1,0:T(8,128)S(1)} %get-tuple-element.9.refs_0_, f32[3,2,2048]{2,1,0:T(2,128)S(1)} %get-tuple-element.10.refs_1_, f32[2,200]{1,0:T(2,128)S(1)} %get-tuple-element.11.refs_2_), custom_call_target="tpu_custom_call" | custom-call | tf_op jit(solution)/shard_map/pallas_call | solution.py:461

commit v4 on v3

--- a/solution.py
+++ b/solution.py
@@ -17,7 +17,8 @@
 WIDE = 256
 CT = 16
 CELLS = CT * 128
-CHUNKS = 8
+CHUNKS = 4
+AHEAD = 4
 CW = CELLS // CHUNKS
 EW = 512
 BF16 = jnp.bfloat16
@@ -89,7 +90,7 @@
         part = pl.ds(pl.multiple_of(k * CW, CW), CW)
         return pltpu.make_async_copy(shp_h.at[:, :, part], shp.at[:, pl.ds(0, MODES), part], csem.at[k])
 
-    for k in range(CHUNKS):
+    for k in range(AHEAD):
         chunk(k).start()
 
     barrier = pltpu.get_barrier_semaphore()
@@ -101,15 +102,13 @@
         for cc in range(NC):
             greet(at(z, x, cc), lax.rem(y + dy, NY))
     for dx in range(1, NX):
-        for cc in range(NC):
-            greet(at(z, lax.rem(x + dx, NX), cc), y)
+        greet(at(z, lax.rem(x + dx, NX), core), y)
     for dz in range(1, NZ):
-        for cc in range(NC):
-            greet(at(lax.rem(z + dz, NZ), x, cc), y)
+        greet(at(lax.rem(z + dz, NZ), x, core), y)
     greet(at(z, x, other), y)
     greet(lax.rem(chip + CHIPS - 1, CHIPS) * NC + 1, y)
     greet(lax.rem(chip + 1, CHIPS) * NC, y)
-    greeted = (NY - 1) * NC + (NX - 1) * NC + (NZ - 1) * NC + 3
+    greeted = (NY - 1) * NC + (NX - 1) + (NZ - 1) + 3
 
     ma[...] = jnp.zeros_like(ma)
     vmsg[...] = jnp.zeros_like(vmsg)
@@ -145,6 +144,12 @@
 
     def project(k, carry):
         chunk(k).wait()
+        if AHEAD < CHUNKS:
+
+            @pl.when(k + AHEAD < CHUNKS)
+            def _():
+                chunk(k + AHEAD).start()
+
         high, low = carry
         for d in range(3):
             part = pl.ds(pl.multiple_of(k * CW, CW), CW)
@@ -177,8 +182,7 @@
     c_jac += [bring(adj_h, adj.at[y], lsem.at[13]), bring(vol_h, vol, lsem.at[14])]
     pl.semaphore_wait(barrier, greeted)
     for dx in range(1, NX):
-        for cc in range(NC):
-            pl.semaphore_signal(ready, inc=1, device_id=(at(z, lax.rem(x + dx, NX), cc), y), device_id_type=MESH)
+        pl.semaphore_signal(ready, inc=1, device_id=(at(z, lax.rem(x + dx, NX), core), y), device_id_type=MESH)
 
     def send(src, dst, ssem, rsem, where, inst):
         copy = pltpu.make_async_remote_copy(
@@ -237,9 +241,12 @@
     down = jnp.sum(jnp.where(eight, slots.astype(F32), 0.0), axis=1, keepdims=True)
     differ = jnp.broadcast_to(down, (8, 8)) - slots.astype(F32)
     h = coupling_of(differ.astype(jnp.int32))
-    own = 2 * y + core
     lanes8 = iota((8, 8), 1)
-    own_h = jnp.sum(jnp.where(lanes8 == own, h, 0.0), axis=1, keepdims=True)
+
+    def column_of(s):
+        return jnp.sum(jnp.where(lanes8 == 2 * y + s, h, 0.0), axis=1, keepdims=True)
+
+    pick = [column_of(s) for s in range(2)]
 
     for n in range(1, NY * NC):
         dy, dc = n // NC, n % NC
@@ -266,23 +273,24 @@
     late = xp[0] + xp[1]
     for a in range(8):
         proj = proj - h[:, a : a + 1] * late[a : a + 1, :]
-    plain = jnp.sum(jnp.where(iota((8, WIDE), 0) == own, proj, 0.0), axis=0, keepdims=True)
-    mixed = jnp.sum(own_h * proj, axis=0, keepdims=True)
-    rhs = plain[:, 0:MODES] + damp[...] * mixed[:, 0:MODES]
     mb[...] = jnp.zeros_like(mb)
-    mb[pl.ds(0, 1), :] = rhs[:, 0:128]
-    mb[pl.ds(1, 1), pl.ds(0, MODES - 128)] = rhs[:, 128:MODES]
-
-    pl.semaphore_wait(ready, (NX - 1) * NC)
+    for s in range(2):
+        plain = jnp.sum(jnp.where(iota((8, WIDE), 0) == 2 * y + s, proj, 0.0), axis=0, keepdims=True)
+        mixed = jnp.sum(pick[s] * proj, axis=0, keepdims=True)
+        rhs = plain[:, 0:MODES] + damp[...] * mixed[:, 0:MODES]
+        mb[pl.ds(s, 1), :] = rhs[:, 0:128]
+        mb[pl.ds(2 + s, 1), pl.ds(0, MODES - 128)] = rhs[:, 128:MODES]
+
+    pl.semaphore_wait(ready, NX - 1)
 
     def hops(offset):
-        dz, dx, _ = offset
+        dz, dx = offset
         return min(dz, NZ - dz) + min(dx, NX - dx)
 
-    offsets = [(dz, dx, dc) for dz in range(NZ) for dx in range(NX) for dc in range(NC)][1:]
-    for n, (dz, dx, dc) in enumerate(sorted(offsets, key=hops, reverse=True)):
-        where = at(lax.rem(z + dz, NZ), lax.rem(x + dx, NX), lax.rem(core + dc, NC))
-        send(mb, bbuf.at[space], bsend.at[n], brecv.at[space], where, y)
+    offsets = [(dz, dx) for dz in range(NZ) for dx in range(NX)][1:]
+    for n, (dz, dx) in enumerate(sorted(offsets, key=hops, reverse=True)):
+        where = at(lax.rem(z + dz, NZ), lax.rem(x + dx, NX), core)
+        send(mb, bbuf.at[chip], bsend.at[n], brecv.at[chip], where, y)
 
     rr[...] = jnp.zeros_like(rr)
     mm[...] = jnp.zeros_like(mm)
@@ -293,7 +301,6 @@
         pltpu.make_async_copy(adj.at[src], adj.at[src], grecv.at[src]).wait()
     lane8, sub8 = iota((8, 128), 1), iota((8, 128), 0)
     parity = lax.rem(sub8, 2)
-    pick = [jnp.sum(jnp.where(lanes8 == 2 * y + s, h, 0.0), axis=1, keepdims=True) for s in range(2)]
 
     def entry(a, s):
         return jnp.broadcast_to(pick[s][a : a + 1, :], (8, 128))
@@ -325,18 +332,13 @@
     for c in sent_a + sent_v + sent_g + sent_h:
         c.wait_send()
 
-    own_sum, other_sum = mb[...], jnp.zeros((2, 128), F32)
-    for dz, dx, dc in sorted(offsets, key=hops):
-        src = at(lax.rem(z + dz, NZ), lax.rem(x + dx, NX), lax.rem(core + dc, NC))
+    total = mb[...]
+    for dz, dx in sorted(offsets, key=hops):
+        src = lax.rem(z + dz, NZ) * NX + lax.rem(x + dx, NX)
         pltpu.make_async_copy(mb, bbuf.at[src], brecv.at[src]).wait()
-        if dc == 0:
-            own_sum = own_sum + bbuf[src]
-        else:
-            other_sum = other_sum + bbuf[src]
-    even = jnp.broadcast_to(core, (2, 128)) == 0
-    for row, total in enumerate((jnp.where(even, own_sum, other_sum), jnp.where(even, other_sum, own_sum))):
-        rr[pl.ds(row, 1), pl.ds(0, 128)] = total[0:1]
-        rr[pl.ds(row, 1), pl.ds(128, 128)] = total[1:2]
+        total = total + bbuf[src]
+    rr[pl.ds(0, 2), pl.ds(0, 128)] = total[0:2]
+    rr[pl.ds(0, 2), pl.ds(128, 128)] = total[2:4]
     modal = jnp.dot(rr[:, pl.ds(0, MODES)], inv[...], precision=HIGHEST, preferred_element_type=F32)
     modal_o[...] = modal[0:2]
     mm[:, pl.ds(0, MODES)] = modal
@@ -353,7 +355,7 @@
         pltpu.make_async_copy(mb, mb, bsend.at[n]).wait()
         return carry
 
-    lax.fori_loop(0, TILES - 1, drain, 0)
+    lax.fori_loop(0, CHIPS - 1, drain, 0)
 
 
 def place(*refs):
@@ -434,8 +436,8 @@
             vmem((4, 2, WIDE), F32),
             vmem((2, 8, WIDE), F32),
             vmem((2, 8, WIDE), F32),
-            vmem((2, 128), F32),
-            vmem((TILES, 2, 128), F32),
+            vmem((4, 128), F32),
+            vmem((CHIPS, 4, 128), F32),
             vmem((8, WIDE), F32),
             vmem((8, WIDE), F32),
             vmem((5, 8, 128), F32),
@@ -451,8 +453,8 @@
             dma((2,)),
             dma((NY,)),
             dma((NY,)),
-            dma((TILES,)),
-            dma((TILES,)),
+            dma((CHIPS,)),
+            dma((CHIPS,)),
         ],
         compiler_params=pltpu.CompilerParams(
             collective_id=0, has_side_effects=True, vmem_limit_bytes=56 * 1024 * 1024

time: 25.9 us -> 23.8 us (0.919)
  Pallas kernels: 25.1 us -> 23 us
    pallas_call x1, Pallas kernels: 24.5 us -> 22.4 us  [shards(): pl.pallas_call(kernel, out_shape=tuple((vmem(shape, F32) for shape in res...]
where the time goes in v4:
time: 23.8 us; the launch traced here: 23.7 us
  Pallas kernels  23 us (97%)
  between operations  0.64 us (3%)
    pallas_call x1, Pallas kernels, shards(): pl.pallas_call(kernel, out_shape=tuple((vmem(shape, F32) for shape in res...  22.4 us
    pallas_call x1, Pallas kernels, shards(): pl.pallas_call(place, out_shape=tuple((jax.ShapeDtypeStruct(shape, F32) f...  0.68 us

profile of v4, /device:TPU:1, one launch (start us, length us, event | category | flops | bytes accessed | tf_op | source)
XLA Modules:
  0.0 23.7 jit_solution(3309509653775746797)
XLA Ops:
  0.6 22.4 %shard_map.130 = (f32[5,32,128]{2,1,0:T(8,128)S(1)}, f32[3,2,2048]{2,1,0:T(2,128)S(1)}, f32[2,200]{1,0:T(2,128)S(1)}) custom-call(f32[5,32,128]{2,1,0:T(8,128)} %bitcast.43, f32[5,2,2048]{2,1,0:T(2,128)} %bitcast.44, f32[5,5,32,128]{3,2,1,0:T(8,128)} %bitcast.37, f32[5,5,32,128]{3,2,1,0:T(8,128)} %bitcast.39, f32[5,5,32,128]{3,2,1,0:T(8,128)} %bitcast.41, ...), custom_call_target="tpu_custom_call" | custom-call | tf_op jit(solution)/shard_map/pallas_call | solution.py:407
  23.0 0.7 %shard_map.131 = (f32[5,32,128]{2,1,0:T(8,128)}, f32[3,2,2048]{2,1,0:T(2,128)}, f32[2,200]{1,0:T(2,128)}) custom-call(f32[5,32,128]{2,1,0:T(8,128)S(1)} %get-tuple-element.9.refs_0_, f32[3,2,2048]{2,1,0:T(2,128)S(1)} %get-tuple-element.10.refs_1_, f32[2,200]{1,0:T(2,128)S(1)} %get-tuple-element.11.refs_2_), custom_call_target="tpu_custom_call" | custom-call | tf_op jit(solution)/shard_map/pallas_call | solution.py:463

commit v5 on v4

--- a/solution.py
+++ b/solution.py
@@ -60,12 +60,11 @@
 def kernel(
     adj_h, adjw_h, jc_h, jl_h, jr_h, jcw_h, jlw_h, jrw_h, vol_h, volw_h, nrm_h, surf_h, imap_h, shp_h, damp_h, inv_h,
     flow_o, mesh_o, modal_o,
-    adj, adjw, jac4, jac, vol, volw, nrm, surf, imap, shp, damp, inv,
+    adj, jac4, jac, vol, volw, nrm, surf, imap, shp, damp, inv,
     vol2, wf, w16, shi, slo, fl, fr, fb,
-    ma, abuf, vmsg, vbuf, xl, xp, mb, bbuf, rr, mm,
-    hl, hr,
+    ma, vm, abuf, xl, xp, mb, bbuf, rr, mm, halo,
     lsem, csem, ready,
-    asend, arecv, vsend, vrecv, hsend, hrecv, gsend, grecv, bsend, brecv,
+    asend, arecv, hsend, hrecv, gsend, grecv, bsend, brecv,
 ):
     space, y = lax.axis_index("space"), lax.axis_index("inst")
     core = lax.rem(space, NC)
@@ -82,9 +81,12 @@
         copy.start()
         return copy
 
-    c_first = [bring(adjw_h, adjw, lsem.at[0])]
-    c_first += [bring(j.at[:, 4], jac4.at[i], lsem.at[1 + i]) for i, j in enumerate((jcw_h, jlw_h, jrw_h))]
-    c_first += [bring(volw_h, volw, lsem.at[4]), bring(surf_h, surf, lsem.at[5]), bring(nrm_h, nrm, lsem.at[6])]
+    def together(ref, sem):
+        pltpu.make_async_copy(ref, ref, sem).wait()
+
+    for i, part in enumerate((jcw_h.at[:, 4], jlw_h.at[:, 4], jrw_h.at[:, 4], adjw_h)):
+        bring(part, jac4.at[i], lsem.at[0])
+    c_first = [bring(volw_h, volw, lsem.at[1]), bring(surf_h, surf, lsem.at[2]), bring(nrm_h, nrm, lsem.at[3])]
 
     def chunk(k):
         part = pl.ds(pl.multiple_of(k * CW, CW), CW)
@@ -111,25 +113,26 @@
     greeted = (NY - 1) * NC + (NX - 1) + (NZ - 1) + 3
 
     ma[...] = jnp.zeros_like(ma)
-    vmsg[...] = jnp.zeros_like(vmsg)
+    vm[...] = jnp.zeros_like(vm)
     wf[...] = jnp.zeros_like(wf)
     for d in range(3):
         shp[d, pl.ds(MODES, ROWS - MODES), :] = jnp.zeros((ROWS - MODES, CELLS), F32)
 
+    together(jac4, lsem.at[0])
     for c in c_first:
         c.wait()
 
     def direct4(i):
-        total = jac4[i, 0] * adjw[0]
+        total = jac4[i, 0] * jac4[3, 0]
         for f in range(1, 5):
-            total = total + jac4[i, f] * adjw[f]
+            total = total + jac4[i, f] * jac4[3, f]
         return total
 
     left4, right4 = direct4(1), direct4(2)
     cell = iota((2, CELLS), 1)
     base4 = direct4(0) + jnp.where(cell == CELLS - 1, 0.0, pltpu.roll(left4, CELLS - 1, 1))
     base4 = base4 + jnp.where(cell == 0, 0.0, pltpu.roll(right4, 1, 1))
-    late4 = volw[...] * adjw[4]
+    late4 = volw[...] * jac4[3, 4]
     walls = surf[...].astype(F32)
     for d in range(3):
         part = pl.ds(d * CELLS, CELLS)
@@ -168,18 +171,17 @@
     both = high + low
     summed = both[0:8] + both[8:16]
     ma[:, pl.ds(0, ROWS)] = summed[0:4]
-    vmsg[:, pl.ds(0, ROWS)] = summed[4:6]
+    vm[pl.ds(0, 2), pl.ds(0, ROWS)] = summed[4:6]
     lanes = iota((2, 128), 1)
     tail = ma[pl.ds(0, 2), pl.ds(128, 128)]
     tail = jnp.where(lanes == MODES - 128, left4[:, 0:1], tail)
     tail = jnp.where(lanes == MODES + 1 - 128, right4[:, CELLS - 1 :], tail)
     ma[pl.ds(0, 2), pl.ds(128, 128)] = tail
 
-    c_imap = bring(imap_h, imap, lsem.at[7])
-    c_damp = bring(damp_h, damp, lsem.at[8])
-    c_inv = bring(inv_h, inv, lsem.at[9])
-    c_jac = [bring(j, jac.at[i], lsem.at[10 + i]) for i, j in enumerate((jc_h, jl_h, jr_h))]
-    c_jac += [bring(adj_h, adj.at[y], lsem.at[13]), bring(vol_h, vol, lsem.at[14])]
+    for i, part in enumerate((jc_h, jl_h, jr_h)):
+        bring(part, jac.at[i], csem.at[0])
+    c_adj = [bring(adj_h, adj.at[y], csem.at[1]), bring(vol_h, vol, csem.at[2])]
+    c_small = [bring(imap_h, imap, lsem.at[1]), bring(damp_h, damp, lsem.at[2]), bring(inv_h, inv, lsem.at[3])]
     pl.semaphore_wait(barrier, greeted)
     for dx in range(1, NX):
         pl.semaphore_signal(ready, inc=1, device_id=(at(z, lax.rem(x + dx, NX), core), y), device_id_type=MESH)
@@ -192,26 +194,24 @@
         return copy
 
     mine = y * NC + core
-    sent_a = []
     for dy, dc in ((2, 0), (2, 1), (1, 0), (3, 0), (1, 1), (3, 1), (0, 1)):
-        n = dy * NC + dc
         cc = lax.rem(core + dc, NC)
-        sent_a.append(send(ma, abuf.at[mine], asend.at[n], arecv.at[mine], at(z, x, cc), lax.rem(y + dy, NY)))
-    sent_v = [send(vmsg, vbuf.at[core], vsend.at[0], vrecv.at[core], at(z, x, other), y)]
+        send(ma, abuf.at[mine], asend, arecv, at(z, x, cc), lax.rem(y + dy, NY))
+    edge = NY * NC
+    send(vm, abuf.at[edge + core], asend, arecv, at(z, x, other), y)
     outer = lax.rem(chip + 2 * core - 1 + CHIPS, CHIPS)
-    slot = 3 - core
     for cc in range(NC):
-        sent_v.append(send(vmsg, vbuf.at[slot], vsend.at[1 + cc], vrecv.at[slot], outer * NC + cc, y))
+        send(vm, abuf.at[edge + 3 - core], asend, arecv, outer * NC + cc, y)
     abuf[pl.ds(mine, 1)] = ma[...][None]
-    vbuf[pl.ds(core, 1)] = vmsg[...][None]
-
-    for c in c_jac:
+    abuf[pl.ds(edge + core, 1)] = vm[...][None]
+
+    together(jac, csem.at[0])
+    for c in c_adj:
         c.wait()
     for s in range(2):
         vol2[pl.ds(s, CT, stride=2), :] = vol[...]
-    sent_g = []
     for dy in range(1, NY):
-        sent_g.append(send(adj.at[y], adj.at[y], gsend.at[dy], grecv.at[y], space, lax.rem(y + dy, NY)))
+        send(adj.at[y], adj.at[y], gsend, grecv, space, lax.rem(y + dy, NY))
 
     def combine(j, e):
         total = j[0, e] * adj[y, 0]
@@ -228,14 +228,11 @@
 
     lax.fori_loop(0, 5, component, 0)
     before, after = lax.rem(space + TILES - 1, TILES), lax.rem(space + 1, TILES)
-    sent_h = [
-        send(fl.at[:, pl.ds(0, 8), :], hr, hsend.at[0], hrecv.at[0], before, y),
-        send(fr.at[:, pl.ds(24, 8), :], hl, hsend.at[1], hrecv.at[1], after, y),
-    ]
-
-    c_imap.wait()
-    c_damp.wait()
-    c_inv.wait()
+    send(fl.at[:, pl.ds(0, 8), :], halo.at[0], hsend, hrecv, before, y)
+    send(fr.at[:, pl.ds(24, 8), :], halo.at[1], hsend, hrecv, after, y)
+
+    for c in c_small:
+        c.wait()
     eight = iota((8, 8), 0) == iota((8, 8), 1)
     slots = jnp.broadcast_to(imap[...], (8, 8))
     down = jnp.sum(jnp.where(eight, slots.astype(F32), 0.0), axis=1, keepdims=True)
@@ -248,13 +245,7 @@
 
     pick = [column_of(s) for s in range(2)]
 
-    for n in range(1, NY * NC):
-        dy, dc = n // NC, n % NC
-        src = lax.rem(y + dy, NY) * NC + lax.rem(core + dc, NC)
-        pltpu.make_async_copy(ma, abuf.at[src], arecv.at[src]).wait()
-    pltpu.make_async_copy(vmsg, vbuf.at[other], vrecv.at[other]).wait()
-    for v in (2, 3):
-        pltpu.make_async_copy(vmsg, vbuf.at[v], vrecv.at[v]).wait()
+    together(abuf.at[pl.ds(0, NY * NC - 1 + 3)], arecv)
     for cc in range(NC):
         for yy in range(NY):
             xl[cc, pl.ds(2 * yy, 2), :] = abuf[yy * NC + cc, pl.ds(0, 2), :]
@@ -263,10 +254,10 @@
     has_after = jnp.where(chip < CHIPS - 1, 1.0, 0.0)
     proj = xl[0] + xl[1]
     edges = (
-        (xl[0][:, 200:201] * has_before, vbuf[2, pl.ds(1, 1), :]),
-        (xl[0][:, 201:202], vbuf[1, pl.ds(0, 1), :]),
-        (xl[1][:, 200:201], vbuf[0, pl.ds(1, 1), :]),
-        (xl[1][:, 201:202] * has_after, vbuf[3, pl.ds(0, 1), :]),
+        (xl[0][:, 200:201] * has_before, abuf[edge + 2, pl.ds(1, 1), :]),
+        (xl[0][:, 201:202], abuf[edge + 1, pl.ds(0, 1), :]),
+        (xl[1][:, 200:201], abuf[edge, pl.ds(1, 1), :]),
+        (xl[1][:, 201:202] * has_after, abuf[edge + 3, pl.ds(0, 1), :]),
     )
     for amount, vector in edges:
         proj = proj + amount * vector
@@ -288,17 +279,15 @@
         return min(dz, NZ - dz) + min(dx, NX - dx)
 
     offsets = [(dz, dx) for dz in range(NZ) for dx in range(NX)][1:]
-    for n, (dz, dx) in enumerate(sorted(offsets, key=hops, reverse=True)):
+    for dz, dx in sorted(offsets, key=hops, reverse=True):
         where = at(lax.rem(z + dz, NZ), lax.rem(x + dx, NX), core)
-        send(mb, bbuf.at[chip], bsend.at[n], brecv.at[chip], where, y)
+        send(mb, bbuf.at[chip], bsend, brecv, where, y)
+    bbuf[pl.ds(chip, 1)] = mb[...][None]
 
     rr[...] = jnp.zeros_like(rr)
     mm[...] = jnp.zeros_like(mm)
-    pltpu.make_async_copy(hr, hr, hrecv.at[0]).wait()
-    pltpu.make_async_copy(hl, hl, hrecv.at[1]).wait()
-    for dy in range(1, NY):
-        src = lax.rem(y + dy, NY)
-        pltpu.make_async_copy(adj.at[src], adj.at[src], grecv.at[src]).wait()
+    together(halo, hrecv)
+    together(adj.at[pl.ds(0, NY - 1)], grecv)
     lane8, sub8 = iota((8, 128), 1), iota((8, 128), 0)
     parity = lax.rem(sub8, 2)
 
@@ -320,23 +309,24 @@
                 timed = timed + here * same[yy] + swapped * cross[yy]
             total = fb[e, part, :] + vol2[part, :] * timed
             if q == 0:
-                moved = pltpu.roll(pltpu.roll(hl[e], 1, 1), 2, 0)
+                moved = pltpu.roll(pltpu.roll(halo[1, e], 1, 1), 2, 0)
                 total = total + jnp.where((sub8 < 2) & (lane8 == 0), moved * leads, 0.0)
             if q == 3:
-                moved = pltpu.roll(pltpu.roll(hr[e], 127, 1), 6, 0)
+                moved = pltpu.roll(pltpu.roll(halo[0, e], 127, 1), 6, 0)
                 total = total + jnp.where((sub8 >= 6) & (lane8 == 127), moved * follows, 0.0)
             flow_o[e, part, :] = total
         return carry
 
     lax.fori_loop(0, 5, finish, 0)
-    for c in sent_a + sent_v + sent_g + sent_h:
-        c.wait_send()
-
-    total = mb[...]
-    for dz, dx in sorted(offsets, key=hops):
-        src = lax.rem(z + dz, NZ) * NX + lax.rem(x + dx, NX)
-        pltpu.make_async_copy(mb, bbuf.at[src], brecv.at[src]).wait()
-        total = total + bbuf[src]
+    together(abuf.at[pl.ds(0, NY * NC - 1 + 3)], asend)
+    together(adj.at[pl.ds(0, NY - 1)], gsend)
+    together(halo, hsend)
+
+    together(bbuf.at[pl.ds(0, CHIPS - 1)], brecv)
+    parts = [bbuf[n] for n in range(CHIPS)]
+    while len(parts) > 1:
+        parts = [parts[i] + parts[i + 1] for i in range(0, len(parts), 2)]
+    total = parts[0]
     rr[pl.ds(0, 2), pl.ds(0, 128)] = total[0:2]
     rr[pl.ds(0, 2), pl.ds(128, 128)] = total[2:4]
     modal = jnp.dot(rr[:, pl.ds(0, MODES)], inv[...], precision=HIGHEST, preferred_element_type=F32)
@@ -351,11 +341,7 @@
             spread = spread + lax.dot_general(lead, slo[d, :, part], plain_dot, preferred_element_type=F32)
             mesh_o[d, :, part] = (spread[0:8] + spread[8:16])[0:2] * surf[:, part].astype(F32)
 
-    def drain(n, carry):
-        pltpu.make_async_copy(mb, mb, bsend.at[n]).wait()
-        return carry
-
-    lax.fori_loop(0, CHIPS - 1, drain, 0)
+    together(bbuf.at[pl.ds(0, CHIPS - 1)], bsend)
 
 
 def place(*refs):
@@ -411,8 +397,7 @@
         out_specs=[pl.BlockSpec(memory_space=pltpu.VMEM)] * 3,
         scratch_shapes=[
             vmem((NY, 5, 32, 128), F32),
-            vmem((5, 2, CELLS), F32),
-            vmem((3, 5, 2, CELLS), F32),
+            vmem((4, 5, 2, CELLS), F32),
             vmem((3, 5, 5, 32, 128), F32),
             vmem((CT, 128), F32),
             vmem((1, CELLS), F32),
@@ -431,31 +416,20 @@
             vmem((5, 32, 128), F32),
             vmem((5, 32, 128), F32),
             vmem((4, WIDE), F32),
-            vmem((NY * NC, 4, WIDE), F32),
-            vmem((2, WIDE), F32),
-            vmem((4, 2, WIDE), F32),
+            vmem((4, WIDE), F32),
+            vmem((NY * NC + 4, 4, WIDE), F32),
             vmem((2, 8, WIDE), F32),
             vmem((2, 8, WIDE), F32),
             vmem((4, 128), F32),
             vmem((CHIPS, 4, 128), F32),
             vmem((8, WIDE), F32),
             vmem((8, WIDE), F32),
-            vmem((5, 8, 128), F32),
-            vmem((5, 8, 128), F32),
-            dma((15,)),
+            vmem((2, 5, 8, 128), F32),
+            dma((4,)),
             dma((CHUNKS,)),
             pltpu.SemaphoreType.REGULAR,
-            dma((NY * NC,)),
-            dma((NY * NC,)),
-            dma((3,)),
-            dma((4,)),
-            dma((2,)),
-            dma((2,)),
-            dma((NY,)),
-            dma((NY,)),
-            dma((CHIPS,)),
-            dma((CHIPS,)),
-        ],
+        ]
+        + [dma] * 8,
         compiler_params=pltpu.CompilerParams(
             collective_id=0, has_side_effects=True, vmem_limit_bytes=56 * 1024 * 1024
         ),

time: 23.8 us -> 22.7 us (0.954)
  Pallas kernels: 23 us -> 22 us
    pallas_call x1, Pallas kernels: 22.4 us -> 21.3 us  [shards(): pl.pallas_call(kernel, out_shape=tuple((vmem(shape, F32) for shape in res...]
where the time goes in v5:
time: 22.7 us; the launch traced here: 22.6 us
  Pallas kernels  22 us (97%)
  between operations  0.64 us (3%)
    pallas_call x1, Pallas kernels, shards(): pl.pallas_call(kernel, out_shape=tuple((vmem(shape, F32) for shape in res...  21.3 us
    pallas_call x1, Pallas kernels, shards(): pl.pallas_call(place, out_shape=tuple((jax.ShapeDtypeStruct(shape, F32) f...  0.68 us

profile of v5, /device:TPU:1, one launch (start us, length us, event | category | flops | bytes accessed | tf_op | source)
XLA Modules:
  0.0 22.6 jit_solution(18258621925482792370)
XLA Ops:
  0.6 21.3 %shard_map.130 = (f32[5,32,128]{2,1,0:T(8,128)S(1)}, f32[3,2,2048]{2,1,0:T(2,128)S(1)}, f32[2,200]{1,0:T(2,128)S(1)}) custom-call(f32[5,32,128]{2,1,0:T(8,128)} %bitcast.43, f32[5,2,2048]{2,1,0:T(2,128)} %bitcast.44, f32[5,5,32,128]{3,2,1,0:T(8,128)} %bitcast.37, f32[5,5,32,128]{3,2,1,0:T(8,128)} %bitcast.39, f32[5,5,32,128]{3,2,1,0:T(8,128)} %bitcast.41, ...), custom_call_target="tpu_custom_call" | custom-call | tf_op jit(solution)/shard_map/pallas_call | solution.py:393
  21.9 0.7 %shard_map.131 = (f32[5,32,128]{2,1,0:T(8,128)}, f32[3,2,2048]{2,1,0:T(2,128)}, f32[2,200]{1,0:T(2,128)}) custom-call(f32[5,32,128]{2,1,0:T(8,128)S(1)} %get-tuple-element.9.refs_0_, f32[3,2,2048]{2,1,0:T(2,128)S(1)} %get-tuple-element.10.refs_1_, f32[2,200]{1,0:T(2,128)S(1)} %get-tuple-element.11.refs_2_), custom_call_target="tpu_custom_call" | custom-call | tf_op jit(solution)/shard_map/pallas_call | solution.py:437

commit v6 on v5

--- a/solution.py
+++ b/solution.py
@@ -20,7 +20,7 @@
 CHUNKS = 4
 AHEAD = 4
 CW = CELLS // CHUNKS
-EW = 512
+EW = 1024
 BF16 = jnp.bfloat16
 
 

time: 22.7 us -> 22.7 us (level)
  no operation moved by 1% of the time
where the time goes in v6:
time: 22.7 us; the launch traced here: 22.6 us
  Pallas kernels  21.9 us (96%)
  between operations  0.64 us (3%)
    pallas_call x1, Pallas kernels, shards(): pl.pallas_call(kernel, out_shape=tuple((vmem(shape, F32) for shape in res...  21.2 us
    pallas_call x1, Pallas kernels, shards(): pl.pallas_call(place, out_shape=tuple((jax.ShapeDtypeStruct(shape, F32) f...  0.68 us

profile of v6, /device:TPU:1, one launch (start us, length us, event | category | flops | bytes accessed | tf_op | source)
XLA Modules:
  0.0 22.6 jit_solution(11716809876071047548)
XLA Ops:
  0.6 21.2 %shard_map.130 = (f32[5,32,128]{2,1,0:T(8,128)S(1)}, f32[3,2,2048]{2,1,0:T(2,128)S(1)}, f32[2,200]{1,0:T(2,128)S(1)}) custom-call(f32[5,32,128]{2,1,0:T(8,128)} %bitcast.43, f32[5,2,2048]{2,1,0:T(2,128)} %bitcast.44, f32[5,5,32,128]{3,2,1,0:T(8,128)} %bitcast.37, f32[5,5,32,128]{3,2,1,0:T(8,128)} %bitcast.39, f32[5,5,32,128]{3,2,1,0:T(8,128)} %bitcast.41, ...), custom_call_target="tpu_custom_call" | custom-call | tf_op jit(solution)/shard_map/pallas_call | solution.py:393
  21.9 0.7 %shard_map.131 = (f32[5,32,128]{2,1,0:T(8,128)}, f32[3,2,2048]{2,1,0:T(2,128)}, f32[2,200]{1,0:T(2,128)}) custom-call(f32[5,32,128]{2,1,0:T(8,128)S(1)} %get-tuple-element.9.refs_0_, f32[3,2,2048]{2,1,0:T(2,128)S(1)} %get-tuple-element.10.refs_1_, f32[2,200]{1,0:T(2,128)S(1)} %get-tuple-element.11.refs_2_), custom_call_target="tpu_custom_call" | custom-call | tf_op jit(solution)/shard_map/pallas_call | solution.py:437
